TPU v7x, 128 devices: a whole 4x4x4 slice. The times are simulated.
128 devices in a mesh: row: 8 (over z, core), col: 16 (over x, y).
Axes of the slice: x: 4, y: 4, z: 4, core: 2. Of those that a mesh axis runs over, the one named last changes fastest.
Arguments:
- factor_strip: float32 [4, 3, 512, 4096], P(None, None, 'col', 'row'), may hold values from -0.4375 to 0.4375
- pivots: float32 [3, 512], replicated, may hold values from 1 to 4
- right_side: float32 [4, 4096, 16384], P(None, 'row', 'col'), may hold values from -6 to 6
Outputs:
- solved: float32 [3, 512, 16384], P(None, None, 'col')
- trailing: float32 [4, 4096, 16384], P(None, 'row', 'col')
All inputs are finite; a program needn't handle non-finite values.
Results may differ from a plain program's by a relative error of at most 0.0001.
Values sent between devices are 32-bit elements; how exact they have to be, the bound alone decides.
No kernel may reach another device: no remote copies, remote signals or barrier semaphores. Data moves between devices by JAX's collectives and lax.ppermute only.
A program may use at most 128 MiB of HBM per device.

v0:
```python
import jax
import jax.numpy as jnp
from jax import lax
from jax.sharding import PartitionSpec as P

PANELS = 3


def from_root(block, axis, source):
    block = jnp.where(lax.axis_index(axis) == source, block, jnp.zeros_like(block))
    return lax.psum(block, axis)


def per_device(factor_strip, pivots, right_side):
    row_index = lax.axis_index("row")
    row_count = lax.axis_size("row")
    sweeps = right_side.shape[0]
    block_ids = jnp.arange(sweeps, dtype=jnp.int32) * row_count + row_index
    gathered = lax.all_gather(factor_strip, "col", axis=2, tiled=True)
    work = right_side
    outputs = []
    for panel_index in range(PANELS):
        panel = gathered[:, panel_index]
        lower = jnp.tril(panel[0].T, -1) + jnp.diag(pivots[panel_index])
        local_solve = jax.scipy.linalg.solve_triangular(lower, work[0], lower=True)
        result = from_root(local_solve, "row", panel_index)
        outputs.append(result)
        update = jnp.einsum("bcr,cn->brn", panel, result, precision=lax.Precision.HIGHEST)
        keep = (block_ids > panel_index)[:, None, None]
        work = jnp.where(keep, work - update, work)
    return (jnp.stack(outputs), work)


def solution(mesh):
    return jax.shard_map(
        per_device,
        mesh=mesh,
        in_specs=(P(None, None, "col", "row"), P(), P(None, "row", "col")),
        out_specs=(P(None, None, "col"), P(None, "row", "col")),
        check_vma=False,
    )
```

profile of v0, /device:TPU:0, one launch (start us, length us, event | category | flops | bytes accessed | tf_op | source)
XLA Modules:
  0.0 468.2 jit_solution(12298712181927813203)
XLA Ops:
  7.2 2.1 copy.5
  9.4 8.7 %copy.11 = f32[4,512,1024]{1,2,0:T(8,128)} copy(f32[4,512,1024]{2,1,0:T(8,128)} %param.7) | data formatting | bytes 16777216 | tf_op args[2]
  19.8 83.1 %all-gather.2.cloned.1.call-done = f32[4,3,512,512]{3,2,0,1:T(8,128)} async-done(((f32[4,3,32,512]{3,2,0,1:T(8,128)}), f32[4,3,512,512]{3,2,0,1:T(8,128)}) %all-gather.2.cloned.1.call-update) | async-done | bytes 12582928 | tf_op jit(solution)/shard_map/all_gather | solution.py:19
  102.9 3.7 fusion.35
  106.6 12.4 %while.6 = (s32[]{:T(128)}, f32[512,512]{0,1:T(8,128)}, s32[4,2]{0,1:T(2,128)S(1)}, f32[4,128,128]{2,1,0:T(8,128)S(1)}, s32[]{:T(128)}) while((s32[]{:T(128)}, f32[512,512]{0,1:T(8,128)}, s32[4,2]{0,1:T(2,128)S(1)}, f32[4,128,128]{2,1,0:T(8,128)S(1)}, s32[]{:T(128)}) %tuple.61), condition=%wide.while_cond, body=%wide.while_body.sunk | while | flops 2 | bytes 393321 | solution.py:25
  107.3 2.3 dynamic-slice.17
  110.4 2.3 dynamic-slice.17
  113.5 2.3 dynamic-slice.17
  116.7 2.2 dynamic-slice.17
  119.7 40.1 %custom-call.5 = f32[4,128,128]{1,2,0:T(8,128)S(1)} custom-call(f32[4,128,128]{2,1,0:T(8,128)} %copy-done.3), custom_call_target="InvertDiagBlocksLowerTriangular" | custom-call | tf_op jit(solution)/shard_map/jit(_solve_triangular)/triangular_solve | solution.py:25
  164.9 2.0 fusion.30
  169.4 11.7 %while.7 = (s32[]{:T(128)}, f32[512,512]{0,1:T(8,128)}, s32[4,2]{0,1:T(2,128)S(1)}, f32[4,128,128]{2,1,0:T(8,128)S(1)}, s32[]{:T(128)}) while((s32[]{:T(128)}, f32[512,512]{0,1:T(8,128)}, s32[4,2]{0,1:T(2,128)S(1)}, f32[4,128,128]{2,1,0:T(8,128)S(1)}, s32[]{:T(128)}) %tuple.78), condition=%wide.while_cond.clone, body=%wide.while_body.clone.sunk | while | flops 2 | bytes 393321 | solution.py:25
  170.1 2.2 dynamic-slice.19
  173.0 2.2 dynamic-slice.19
  176.0 2.2 dynamic-slice.19
  178.9 2.1 dynamic-slice.19
  181.1 39.3 %custom-call.6 = f32[4,128,128]{1,2,0:T(8,128)S(1)} custom-call(f32[4,128,128]{2,1,0:T(8,128)S(1)} %get-tuple-element.24), custom_call_target="InvertDiagBlocksLowerTriangular" | custom-call | tf_op jit(solution)/shard_map/jit(_solve_triangular)/triangular_solve | solution.py:25
  220.5 14.8 %all-reduce.4.cloned.1.call-done = f32[512,1024]{1,0:T(8,128)} async-done(((f32[512,1024]{1,0:T(8,128)}), f32[512,1024]{1,0:T(8,128)}) %all-reduce.4.cloned.1.call-update) | async-done | bytes 2097168 | tf_op jit(solution)/shard_map/psum | solution.py:11
  235.3 18.9 %subtract_select_fusion.2 = f32[4,512,1024]{1,2,0:T(8,128)S(1)} fusion(f32[4,512,1024]{1,2,0:T(8,128)} %copy.11, pred[4]{0:T(512)(128)(4,1)S(1)} %broadcast_compare_fusion.2, f32[4,3,512,512]{3,2,0,1:T(8,128)} %all-gather.2.cloned.1.call-done, f32[512,1024]{1,0:T(8,128)} %all-reduce.4.cloned.1.call-done), kind=kOutput, calls=%fused_computation.8 | convolution fusion | flops 12889096192 | bytes 23068676 | tf_op jit(solution)/shard_map/bcr,cn->brn/dot_general | solution.py:28
  255.1 1.9 convolution_subtract_fusion.4
  257.6 2.7 convolution_subtract_fusion.1
  261.0 3.7 fusion.27
  267.1 9.3 %while.8 = (s32[]{:T(128)}, f32[512,512]{0,1:T(8,128)S(1)}, s32[4,2]{0,1:T(2,128)S(1)}, f32[4,128,128]{2,1,0:T(8,128)S(1)}, s32[]{:T(128)}) while((s32[]{:T(128)}, f32[512,512]{0,1:T(8,128)S(1)}, s32[4,2]{0,1:T(2,128)S(1)}, f32[4,128,128]{2,1,0:T(8,128)S(1)}, s32[]{:T(128)}) %tuple.79), condition=%wide.while_cond.clone.1, body=%wide.while_body.clone.1.sunk | while | flops 2 | bytes 393321 | solution.py:25
  276.4 39.3 %custom-call.7 = f32[4,128,128]{1,2,0:T(8,128)S(1)} custom-call(f32[4,128,128]{2,1,0:T(8,128)S(1)} %get-tuple-element.25), custom_call_target="InvertDiagBlocksLowerTriangular" | custom-call | tf_op jit(solution)/shard_map/jit(_solve_triangular)/triangular_solve | solution.py:25
  315.7 17.3 %all-reduce.6.cloned.1.call-done = f32[512,1024]{1,0:T(8,128)} async-done(((f32[512,1024]{1,0:T(8,128)}), f32[512,1024]{1,0:T(8,128)}) %all-reduce.6.cloned.1.call-update) | async-done | bytes 2097168 | tf_op jit(solution)/shard_map/psum | solution.py:11
  333.0 18.9 %subtract_select_fusion.1 = f32[4,512,1024]{1,2,0:T(8,128)S(1)} fusion(f32[4,512,1024]{1,2,0:T(8,128)} %copy-done, pred[4]{0:T(512)(128)(4,1)S(1)} %broadcast_compare_fusion.1, f32[4,3,512,512]{3,2,0,1:T(8,128)} %all-gather.2.cloned.1.call-done, f32[512,1024]{1,0:T(8,128)} %all-reduce.6.cloned.1.call-done), kind=kOutput, calls=%fused_computation.7 | convolution fusion | flops 12889096192 | bytes 23068676 | tf_op jit(solution)/shard_map/bcr,cn->brn/dot_general | solution.py:28
  354.4 1.8 convolution_subtract_fusion
  356.9 2.8 fusion.24
  361.9 65.5 %all-reduce.8.cloned.1.call-done = f32[512,1024]{1,0:T(8,128)} async-done(((f32[512,1024]{1,0:T(8,128)}), f32[512,1024]{1,0:T(8,128)}) %all-reduce.8.cloned.1.call-update) | async-done | bytes 2097168 | tf_op jit(solution)/shard_map/psum | solution.py:11
  427.4 19.3 %subtract_select_fusion = f32[4,512,1024]{1,2,0:T(8,128)} fusion(f32[4,512,1024]{1,2,0:T(8,128)} %copy-done.1, pred[4]{0:T(512)(128)(4,1)S(1)} %broadcast_compare_fusion, f32[4,3,512,512]{3,2,0,1:T(8,128)} %all-gather.2.cloned.1.call-done, f32[512,1024]{1,0:T(8,128)} %all-reduce.8.cloned.1.call-done), kind=kOutput, calls=%fused_computation.6 | convolution fusion | flops 12889096192 | bytes 23068676 | tf_op jit(solution)/shard_map/bcr,cn->brn/dot_general | solution.py:28
  446.7 8.8 %copy.16 = f32[4,512,1024]{2,1,0:T(8,128)} copy(f32[4,512,1024]{1,2,0:T(8,128)} %subtract_select_fusion) | data formatting | bytes 16777216
  455.5 5.9 %pad_maximum_fusion = f32[3,512,1024]{2,1,0:T(8,128)} fusion(f32[1,512,1024]{2,1,0:T(8,128)} %bitcast.156, f32[1,512,1024]{2,1,0:T(8,128)} %bitcast.155, f32[1,512,1024]{2,1,0:T(8,128)S(1)} %bitcast.154), kind=kLoop, calls=%fused_computation.9 | loop fusion | flops 3145728 | bytes 12582912 | tf_op jit(solution)/shard_map/stack | solution.py:31
  (101 shorter events, 34.5 us)
Async XLA Ops:
  7.2 95.7 %all-gather.2.cloned.1.call-start = ((), (), s32[]{:S(2)}) async-start(), calls=%async_computation | async-start | bytes 13369344 | tf_op jit(solution)/shard_map/all_gather | solution.py:19
  9.3 226.0 %all-reduce.4.cloned.1.call-start = ((), (), s32[]{:S(2)}) async-start(), calls=%async_computation.1 | async-start | bytes 4194304 | tf_op jit(solution)/shard_map/psum | solution.py:11
  9.4 8.7 %copy-start.4 = (f32[3,512]{1,0:T(4,128)S(1)}, f32[3,512]{1,0:T(4,128)}, u32[]{:S(2)}) copy-start(f32[3,512]{1,0:T(4,128)} %param.6) | copy-start | bytes 18436
  119.0 0.7 copy-start.3
  169.1 163.9 %all-reduce.6.cloned.1.call-start = ((), (), s32[]{:S(2)}) async-start(), calls=%async_computation.2 | async-start | bytes 4194304 | tf_op jit(solution)/shard_map/psum | solution.py:11
  254.2 10.6 %copy-start = (f32[4,512,1024]{1,2,0:T(8,128)}, f32[4,512,1024]{1,2,0:T(8,128)S(1)}, u32[]{:S(2)}) copy-start(f32[4,512,1024]{1,2,0:T(8,128)S(1)} %subtract_select_fusion.2) | copy-start | bytes 25165828
  267.0 160.4 %all-reduce.8.cloned.1.call-start = ((), (), s32[]{:S(2)}) async-start(), calls=%async_computation.3 | async-start | bytes 4194304 | tf_op jit(solution)/shard_map/psum | solution.py:11
  351.9 7.8 %copy-start.1 = (f32[4,512,1024]{1,2,0:T(8,128)}, f32[4,512,1024]{1,2,0:T(8,128)S(1)}, u32[]{:S(2)}) copy-start(f32[4,512,1024]{1,2,0:T(8,128)S(1)} %subtract_select_fusion.1) | copy-start | bytes 25165828
  446.7 8.8 %copy-start.2 = (f32[512,1024]{1,0:T(8,128)S(1)}, f32[512,1024]{1,0:T(8,128)}, u32[]{:S(2)}) copy-start(f32[512,1024]{1,0:T(8,128)} %all-reduce.4.cloned.1.call-done) | copy-start | bytes 6291460
Sparse Core Ops, SparseCore 0:
  10.7 92.1 all-gather.1
  169.2 66.0 all-reduce.3
  267.1 65.8 all-reduce.5
  362.0 65.3 all-reduce.7
where the time goes:
time: 476 us; the launch traced here: 468 us
  waiting for transfers between devices  181 us (38%)
  other arithmetic  133 us (28%)
  matrix products  83.8 us (18%)
  local copies, waits for them, and re-layouts  54.9 us (12%)
  between operations  14.3 us (3%)
    another operation x5, other arithmetic, per_device(): local_solve = jax.scipy.linalg.solve_triangular(lower, work[0], lower=True)  122 us
    psum x3, waiting for transfers between devices, from_root(): return lax.psum(block, axis)  97.6 us
    all_gather x1, waiting for transfers between devices, per_device(): gathered = lax.all_gather(factor_strip, 'col', axis=2, tiled=True)  83.1 us
    dot_general x3, matrix products, per_device(): jnp.einsum('bcr,cn->brn', panel, result, precision=lax.Precision.HIGHEST)  57 us
    another operation x64, local copies, waits for them, and re-layouts, per_device(): local_solve = jax.scipy.linalg.solve_triangular(lower, work[0], lower=True)  32.6 us
    another operation x21, matrix products, per_device(): local_solve = jax.scipy.linalg.solve_triangular(lower, work[0], lower=True)  26.8 us
    unnamed x13, local copies, waits for them, and re-layouts  20.3 us
  transfers between devices with their start and end apart: 4, of which 4 were waited for; matrix products, arithmetic and copies ran while one was open for 23% of the time, Pallas kernels for 0%

commit v1 on v0

v1 whole, which is shorter than its diff:
```python
import functools

import jax
import jax.numpy as jnp
from jax import lax
from jax.experimental import pallas as pl
from jax.experimental.pallas import tpu as pltpu
from jax.sharding import PartitionSpec as P


F32, BF16 = jnp.float32, jnp.bfloat16
PANELS, PANEL, SHARE, HALF, NCOL = 3, 512, 32, 512, 1024
AXES = ("row", "col")
TN = (((0,), (0,)), ((), ()))
NN = (((1,), (0,)), ((), ()))

X1, X3, Y1, Y3 = 4, 12, 1, 3
STEPS = {
    (0, 0): (X1, X3, Y1, Y3),
    (0, 1): (Y1, Y3, X1, X3),
    (1, 0): (X3, X1, Y3, Y1),
    (1, 1): (Y3, Y1, X3, X1),
}
OFFSETS = (0, 3, 1, 2)


def permute(value, target):
    pairs = []
    for row in range(8):
        for col in range(16):
            r, c = target(row, col)
            pairs.append((row * 16 + col, r * 16 + c))
    return lax.ppermute(value, AXES, pairs)


def xor_wave(value, color, k):
    return permute(value, lambda r, c: (r, c ^ STEPS[(r % 2, color)][k]))


def swap_cores(value):
    return permute(value, lambda r, c: (r ^ 1, c))


def z_xor(value, mask):
    return permute(value, lambda r, c: (r ^ (2 * mask), c))


def z_ring(value):
    def target(r, c):
        z, core = r // 2, r % 2
        return ((z + (1 if core == 0 else 3)) % 4) * 2 + core, c

    return permute(value, target)


def shift(value, phase, s):
    def target(r, c):
        x, y = c // 4, c % 4
        if (r % 2 + phase) % 2 == 0:
            x = (x + s) % 4
        else:
            y = (y + s) % 4
        return r, x * 4 + y

    return permute(value, target)


def split(v):
    hi = v.astype(BF16)
    return hi, (v - hi.astype(F32)).astype(BF16)


def dot3(a, b, dims):
    ah, al = a
    bh, bl = b
    out = lax.dot_general(ah, bh, dims, preferred_element_type=F32)
    out += lax.dot_general(ah, bl, dims, preferred_element_type=F32)
    out += lax.dot_general(al, bh, dims, preferred_element_type=F32)
    return out


BLOCK = {(0, 0): 0, (0, 2): 1, (1, 2): 2, (0, 1): 3, (1, 1): 4, (2, 2): 5}


def join_body(groups, *refs):
    count = sum(len(g) for g in groups)
    ins, outs, sem = refs[:count], refs[count:-1], refs[-1]
    copies, k = [], 0
    for g, out in zip(groups, outs):
        at = 0
        for n in g:
            copies.append(pltpu.make_async_copy(ins[k], out.at[pl.ds(at, n)], sem))
            at += n
            k += 1
    for c in copies:
        c.start()
    for c in copies:
        c.wait()


def join(*groups):
    flat = [v for g in groups for v in g]
    sizes = tuple(tuple(v.shape[0] for v in g) for g in groups)
    outs = [jax.ShapeDtypeStruct((sum(n),) + g[0].shape[1:], F32) for n, g in zip(sizes, groups)]
    size = sum(v.size for v in flat) * 4
    return pl.pallas_call(
        functools.partial(join_body, sizes),
        out_shape=outs,
        in_specs=[pl.BlockSpec(memory_space=pl.ANY)] * len(flat),
        out_specs=[pl.BlockSpec(memory_space=pltpu.VMEM)] * len(outs),
        scratch_shapes=[pltpu.SemaphoreType.DMA],
        compiler_params=pltpu.CompilerParams(vmem_limit_bytes=size + (1 << 20)),
        cost_estimate=pl.CostEstimate(flops=0, bytes_accessed=2 * size, transcendentals=0),
    )(*flat)


def pack_body(tab, *refs):
    ins, out, sem = refs[:4], refs[4], refs[5]
    copies = []
    for k in range(4):
        for j in range(4):
            src = pl.ds(pl.multiple_of(tab[4 + 4 * k + j] * SHARE, SHARE), SHARE)
            copies.append(pltpu.make_async_copy(ins[k].at[j], out.at[:, src, :], sem))
    for c in copies:
        c.start()
    for c in copies:
        c.wait()


def pack(tab, parts):
    size = PANELS * PANEL * PANEL * 4
    return pl.pallas_call(
        pack_body,
        out_shape=jax.ShapeDtypeStruct((PANELS, PANEL, PANEL), F32),
        in_specs=[pl.BlockSpec(memory_space=pltpu.SMEM)] + [pl.BlockSpec(memory_space=pl.ANY)] * 4,
        out_specs=pl.BlockSpec(memory_space=pltpu.VMEM),
        scratch_shapes=[pltpu.SemaphoreType.DMA],
        compiler_params=pltpu.CompilerParams(vmem_limit_bytes=size + (1 << 20)),
        cost_estimate=pl.CostEstimate(flops=0, bytes_accessed=2 * size, transcendentals=0),
        name="pack",
    )(tab, *parts)


def prep_body(tab, piv, own, other, lh_o, ll_o, vh_o, vl_o, lv, lh, ll, vh, vl, sem):
    core = tab[0]
    ca = pltpu.make_async_copy(own, lv.at[pl.ds(3 * core, 3)], sem.at[0])
    cb = pltpu.make_async_copy(other, lv.at[pl.ds(3 - 3 * core, 3)], sem.at[1])
    ca.start()
    cb.start()
    ca.wait()
    cb.wait()
    for n in range(6):
        hi, lo = split(lv[n])
        lh[n] = hi
        ll[n] = lo
    outs = [pltpu.make_async_copy(a, b, sem.at[2 + k])
            for k, (a, b) in enumerate(((lh, lh_o), (ll, ll_o), (vh, vh_o), (vl, vl_o)))]
    outs[0].start()
    outs[1].start()

    row32 = lax.broadcasted_iota(jnp.int32, (32, 128), 0)
    lane = lax.broadcasted_iota(jnp.int32, (32, 128), 1)
    group = lane // 32
    eye = jnp.where(lane % 32 == row32, 1.0, 0.0).astype(F32)
    r128 = lax.broadcasted_iota(jnp.int32, (128, 128), 0)
    c128 = lax.broadcasted_iota(jnp.int32, (128, 128), 1)
    blocks = [(p, d) for p in range(PANELS) for d in range(4)]
    comp, ts, pvs, vs = [], [], [], []
    for p, d in blocks:
        u = lv[BLOCK[(p, p)], 128 * d:128 * d + 128, 128 * d:128 * d + 128]
        c = jnp.zeros((32, 128), F32)
        for b in range(4):
            c = jnp.where(group == b, u[32 * b:32 * b + 32, :], c)
        comp.append(c)
        ts.append(eye)
        pvs.append(1.0 / jnp.broadcast_to(piv[p:p + 1, 128 * d:128 * d + 128], (8, 128)))
        vs.append(jnp.zeros((32, 128), F32))
    for j in range(31, -1, -1):
        idx = group * 32 + j
        for n in range(len(blocks)):
            pj = jnp.take_along_axis(pvs[n], idx[:8], axis=1)
            vj = jnp.broadcast_to(ts[n][j:j + 1, :] * pj[0:1, :], (32, 128))
            vs[n] = jnp.where(row32 == j, vj, vs[n])
            if j:
                uj = jnp.take_along_axis(comp[n], idx, axis=1)
                ts[n] = jnp.where(row32 < j, ts[n] - uj * vj, ts[n])
    full = [jnp.concatenate([jnp.where(group == b, v, 0.0) for b in range(4)], 0) for v in vs]
    for s in (32, 64):
        off = (r128 // (2 * s) == c128 // (2 * s)) & (r128 // s % 2 == 0) & (c128 // s % 2 == 1)
        ms = []
        for n, (p, d) in enumerate(blocks):
            u = lv[BLOCK[(p, p)], 128 * d:128 * d + 128, 128 * d:128 * d + 128]
            ms.append(dot3(split(jnp.where(off, u, 0.0)), split(full[n]), NN))
        full = [v - dot3(split(v), split(m), NN) for v, m in zip(full, ms)]
    for n, (p, d) in enumerate(blocks):
        hi, lo = split(full[n])
        vh[p, d] = hi
        vl[p, d] = lo
    outs[2].start()
    outs[3].start()
    for c in outs:
        c.wait()


def prep(tab, pivots, own, other):
    hbm = pl.BlockSpec(memory_space=pl.ANY)
    vmem = pl.BlockSpec(memory_space=pltpu.VMEM)
    big = jax.ShapeDtypeStruct((6, PANEL, PANEL), BF16)
    small = jax.ShapeDtypeStruct((PANELS, 4, 128, 128), BF16)
    return pl.pallas_call(
        prep_body,
        out_shape=[big, big, small, small],
        in_specs=[pl.BlockSpec(memory_space=pltpu.SMEM), vmem, hbm, hbm],
        out_specs=[pl.BlockSpec(memory_space=pltpu.HBM)] * 4,
        scratch_shapes=[
            pltpu.VMEM((6, PANEL, PANEL), F32),
            pltpu.VMEM((6, PANEL, PANEL), BF16),
            pltpu.VMEM((6, PANEL, PANEL), BF16),
            pltpu.VMEM((PANELS, 4, 128, 128), BF16),
            pltpu.VMEM((PANELS, 4, 128, 128), BF16),
            pltpu.SemaphoreType.DMA((6,)),
        ],
        compiler_params=pltpu.CompilerParams(vmem_limit_bytes=56 << 20),
        cost_estimate=pl.CostEstimate(flops=4 << 30, bytes_accessed=14 << 20, transcendentals=0),
        name="prep",
    )(tab, pivots, own, other)


def solve_body(tab, lh_h, ll_h, vh_h, vl_h, rhs, swp, r1, r2, r3, r4, out,
               lh, ll, vh, vl, rv, xh, xl, sem_l, sem_v, sem_r):
    core = tab[0]
    cands = [rhs.at[0, :, pl.ds(pl.multiple_of(core * HALF, HALF), HALF)], swp, r1, r2, r3, r4]
    vcopies = [pltpu.make_async_copy(vh_h, vh, sem_v), pltpu.make_async_copy(vl_h, vl, sem_v)]
    lcopies = {}
    for q in range(PANELS):
        for p in range(q + 1):
            n = BLOCK[(p, q)]
            lcopies[(p, q)] = [pltpu.make_async_copy(lh_h.at[n], lh.at[n], sem_l.at[n]),
                               pltpu.make_async_copy(ll_h.at[n], ll.at[n], sem_l.at[n])]
    for q in range(PANELS):
        for k, cand in enumerate(cands):
            @pl.when(tab[1 + q] == k)
            def _():
                pltpu.make_async_copy(cand.at[pl.ds(0, PANEL)], rv.at[q], sem_r.at[q]).start()
        if q == 0:
            for c in vcopies:
                c.start()
        for p in range(q + 1):
            for c in lcopies[(p, q)]:
                c.start()
    for c in vcopies:
        c.wait()
    for q in range(PANELS):
        pltpu.make_async_copy(r1.at[pl.ds(0, PANEL)], rv.at[q], sem_r.at[q]).wait()
        for p in range(q + 1):
            for c in lcopies[(p, q)]:
                c.wait()
        diag = BLOCK[(q, q)]
        for h in range(2):
            cols = slice(256 * h, 256 * h + 256)
            acc = rv[q, :, cols]
            for p in range(q):
                n = BLOCK[(p, q)]
                acc = acc - dot3((lh[n], ll[n]), (xh[p, :, cols], xl[p, :, cols]), TN)
            rv[q, :, cols] = acc
        for i in range(4):
            rows = slice(128 * i, 128 * i + 128)
            for h in range(2):
                cols = slice(256 * h, 256 * h + 256)
                t = rv[q, rows, cols]
                if i:
                    t = t - dot3((lh[diag, 0:128 * i, rows], ll[diag, 0:128 * i, rows]),
                                 (xh[q, 0:128 * i, cols], xl[q, 0:128 * i, cols]), TN)
                x = dot3((vh[q, i], vl[q, i]), split(t), TN)
                hi, lo = split(x)
                xh[q, rows, cols] = hi
                xl[q, rows, cols] = lo
                out[q, rows, cols] = x


def solve(tab, factors, rhs, swp, recvs):
    hbm = pl.BlockSpec(memory_space=pltpu.HBM)
    vmem = pl.BlockSpec(memory_space=pltpu.VMEM)
    return pl.pallas_call(
        solve_body,
        out_shape=jax.ShapeDtypeStruct((PANELS, PANEL, HALF), F32),
        in_specs=[pl.BlockSpec(memory_space=pltpu.SMEM)] + [hbm] * 10,
        out_specs=vmem,
        scratch_shapes=[
            pltpu.VMEM((6, PANEL, PANEL), BF16),
            pltpu.VMEM((6, PANEL, PANEL), BF16),
            pltpu.VMEM((PANELS, 4, 128, 128), BF16),
            pltpu.VMEM((PANELS, 4, 128, 128), BF16),
            pltpu.VMEM((PANELS, PANEL, HALF), F32),
            pltpu.VMEM((PANELS, PANEL, HALF), BF16),
            pltpu.VMEM((PANELS, PANEL, HALF), BF16),
            pltpu.SemaphoreType.DMA((6,)),
            pltpu.SemaphoreType.DMA,
            pltpu.SemaphoreType.DMA((PANELS,)),
        ],
        compiler_params=pltpu.CompilerParams(vmem_limit_bytes=56 << 20),
        cost_estimate=pl.CostEstimate(flops=8 << 30, bytes_accessed=14 << 20, transcendentals=0),
        name="solve",
    )(tab, *factors, rhs, swp, *recvs)


def update_body(tab_ref, xa_hbm, xb_hbm, *refs):
    bufs = (refs[:4], refs[4:8])
    work_ref, out_ref, solved, xv, xh, xl, fv, sem_x, sem_f = refs[8:]
    step = pl.program_id(0)
    b = step // 2
    core = tab_ref[0]
    row = tab_ref[1]
    xc = [pltpu.make_async_copy(src, xv.at[:, :, pl.ds(pl.multiple_of(h * HALF, HALF), HALF)], sem_x.at[k])
          for k, (src, h) in enumerate(((xa_hbm, core), (xb_hbm, 1 - core)))]
    out_copy = pltpu.make_async_copy(xv, solved, sem_x.at[2])

    def fcopies(color, inner, slot):
        for q in range(4):
            for i in range(4):
                s = pl.ds(pl.multiple_of(tab_ref[2 + color * 16 + q * 4 + i] * SHARE, SHARE), SHARE)
                yield pltpu.make_async_copy(bufs[color][q].at[i, inner], fv.at[slot, :, s, :], sem_f.at[slot])

    def start(which, slot):
        for color in range(2):
            for inner in range(2):
                @pl.when(which == color * 2 + inner)
                def _():
                    for c in fcopies(color, inner, slot):
                        c.start()

    slot = lax.rem(b, 2)

    @pl.when(step == 0)
    def _():
        for c in xc:
            c.start()
        start(0, 0)
        start(1, 1)
        for c in xc:
            c.wait()
        out_copy.start()
        for p in range(PANELS):
            hi, lo = split(xv[p])
            xh[p * PANEL:p * PANEL + PANEL, :] = hi
            xl[p * PANEL:p * PANEL + PANEL, :] = lo

    @pl.when(lax.rem(step, 2) == 0)
    def _():
        for c in fcopies(0, 0, slot):
            c.wait()

    cols = pl.ds(pl.multiple_of(lax.rem(step, 2) * 256, 256), 256)
    fs = []
    for p in range(PANELS):
        keep = jnp.logical_or(b > 0, row > p)
        fs.append(jnp.where(keep, fv[slot, p, :, cols], 0.0))
    up = dot3(split(jnp.concatenate(fs, 0)), (xh[...], xl[...]), TN)
    out_ref[0] = work_ref[0] - up

    @pl.when((lax.rem(step, 2) == 1) & (b + 2 < 4))
    def _():
        start(b + 2, slot)

    @pl.when(step == 7)
    def _():
        out_copy.wait()


def update(tab, xa, xb, bufs_a, bufs_b, work):
    wspec = pl.BlockSpec((1, 256, NCOL), lambda s, t: (s // 2, s % 2, 0))
    hbm = pl.BlockSpec(memory_space=pltpu.HBM)
    return pl.pallas_call(
        update_body,
        out_shape=[jax.ShapeDtypeStruct(work.shape, F32), jax.ShapeDtypeStruct((PANELS, PANEL, NCOL), F32)],
        grid_spec=pltpu.PrefetchScalarGridSpec(
            num_scalar_prefetch=1, grid=(8,),
            in_specs=[hbm] * 10 + [wspec],
            out_specs=[wspec, pl.BlockSpec(memory_space=pltpu.HBM)],
            scratch_shapes=[
                pltpu.VMEM((PANELS, PANEL, NCOL), F32),
                pltpu.VMEM((PANELS * PANEL, NCOL), BF16),
                pltpu.VMEM((PANELS * PANEL, NCOL), BF16),
                pltpu.VMEM((2, PANELS, PANEL, PANEL), F32),
                pltpu.SemaphoreType.DMA((3,)),
                pltpu.SemaphoreType.DMA((2,)),
            ],
        ),
        compiler_params=pltpu.CompilerParams(vmem_limit_bytes=60 << 20),
        cost_estimate=pl.CostEstimate(flops=20 << 30, bytes_accessed=42 << 20, transcendentals=0),
        name="update",
    )(tab, xa, xb, *bufs_a, *bufs_b, work)


def table(core, make):
    a = jnp.array(make(0), jnp.int32)
    b = jnp.array(make(1), jnp.int32)
    return jnp.where(core == 0, a, b)


def wave_masks(core, color):
    m = STEPS[(core, color)]
    low = [(m[0] if i & 1 else 0) ^ (m[1] if i & 2 else 0) for i in range(4)]
    return low, [v ^ m[2] for v in low], [v ^ m[3] for v in low], [v ^ m[2] ^ m[3] for v in low]


def panels(factor, pivots, rhs):
    row = lax.axis_index("row")
    col = lax.axis_index("col")
    core, z = row % 2, row // 2
    x, y = col // 4, col % 4
    first = core == 0

    swl = swap_cores(factor[0, 2])
    half_a, half_b = factor[0:2][None], factor[2:4][None]
    ra1 = xor_wave(half_a, 0, 0)
    pay = factor[0, 0:2]
    pay = jnp.where((core == 1) & (z == 1), jnp.broadcast_to(swl[None], pay.shape), pay)
    got = z_xor(pay, 1)
    low = jnp.where(z == 0, pay, got)
    high = jnp.where(z == 0, got, pay)
    share = jnp.where(first, jnp.stack([low[0], high[0], high[1]]), jnp.stack([low[0], low[1], high[0]]))

    slab = rhs[0]
    theirs = jnp.where(first, slab[:, HALF:], slab[:, :HALF])
    mine = jnp.where(first, slab[:, :HALF], slab[:, HALF:])
    swp = swap_cores(theirs)
    rb1 = xor_wave(half_b, 1, 0)
    share = jnp.where(z < 2, share, z_xor(share, 3))

    r1 = z_ring(jnp.where(first, mine, swp))
    r2 = z_ring(jnp.where(z == 0, jnp.where(first, swp, mine), r1))
    r3 = z_ring(jnp.where((z == 0) & (core == 1), r1, r2))
    r4 = z_ring(r3)

    def place(which):
        cols = []
        for k in range(4):
            for j in range(4):
                if which == 0:
                    cols.append((x + OFFSETS[j]) % 4 * 4 + (y + OFFSETS[k]) % 4)
                else:
                    cols.append((x + OFFSETS[k]) % 4 * 4 + (y + OFFSETS[j]) % 4)
        return jnp.stack(cols)

    rtab = jnp.array([[[0, 1, 4], [2, 3, 0], [3, 4, 2], [4, 5, 3]],
                      [[1, 0, 2], [4, 5, 1], [3, 4, 5], [2, 3, 4]]], jnp.int32)
    stab = jnp.concatenate([core[None], rtab[core, z], jnp.where(first, place(0), place(1))]).astype(jnp.int32)

    one = share[None]
    (ph1,) = join([one] + [shift(one, 0, s) for s in (1, 3, 2)])
    lown = pack(stab, [ph1] + [shift(ph1, 1, s) for s in (1, 3, 2)])
    loth = swap_cores(lown)

    fa, fb = join([half_a, ra1], [half_b, rb1])
    ra2, rb2 = xor_wave(fa, 0, 1), xor_wave(fb, 1, 1)
    fa, fb = join([fa, ra2], [fb, rb2])
    ga, gb = xor_wave(fa, 0, 2), xor_wave(fb, 1, 2)
    ha, hb = xor_wave(fa, 0, 3), xor_wave(fb, 1, 3)
    ka, kb = xor_wave(ga, 0, 3), xor_wave(gb, 1, 3)

    factors = prep(stab, pivots, lown, loth)
    xa = solve(stab, factors, rhs, swp, (r1, r2, r3, r4))
    xb = swap_cores(xa)

    def make(c):
        return [v for color in range(2) for part in wave_masks(c, color) for v in part]

    utab = jnp.concatenate([core[None], row[None], table(core, make) ^ col]).astype(jnp.int32)
    work, solved = update(utab, xa, xb, (fa, ga, ha, ka), (fb, gb, hb, kb), rhs)
    return solved, work


def solution(mesh):
    return jax.shard_map(
        panels,
        mesh=mesh,
        in_specs=(P(None, None, "col", "row"), P(), P(None, "row", "col")),
        out_specs=(P(None, None, "col"), P(None, "row", "col")),
        check_vma=False,
    )
```

time: 476 us -> 218 us (0.46); the launches traced: 468 us -> 217 us
  other arithmetic: 133 us -> 7 us
  matrix products: 83.8 us -> 0 us
  waiting for transfers between devices: 181 us -> 110 us
  Pallas kernels: 0 us -> 62.7 us
  local copies, waits for them, and re-layouts: 54.9 us -> 5.5 us
  starting transfers between devices: 0.37 us -> 30.1 us
  between operations: 14.3 us -> 1.12 us
    another operation x6 -> x0, other arithmetic: 128 us -> none  [the longest x5 122 us: per_device(): local_solve = jax.scipy.linalg.solve_triangular(lower, work[0], lower=True)]
    ppermute x0 -> x26, waiting for transfers between devices: none -> 110 us  [permute(): return lax.ppermute(value, AXES, pairs)]
    psum x3 -> x0, waiting for transfers between devices: 97.6 us -> none  [from_root(): return lax.psum(block, axis)]
    all_gather x1 -> x0, waiting for transfers between devices: 83.1 us -> none  [per_device(): gathered = lax.all_gather(factor_strip, 'col', axis=2, tiled=True)]
    pallas_call x0 -> x7, Pallas kernels: none -> 62.7 us  [the longest x1 30.4 us: update(): pl.pallas_call(update_body, out_shape=[jax.ShapeDtypeStruct(work.shape, F...]
    dot_general x3 -> x0, matrix products: 57 us -> none  [per_device(): jnp.einsum('bcr,cn->brn', panel, result, precision=lax.Precision.HIGHEST)]
    another operation x64 -> x2, local copies, waits for them, and re-layouts: 32.6 us -> 0.19 us  [place(): return jnp.stack(cols)]
    ppermute x0 -> x26, starting transfers between devices: none -> 30.1 us  [permute(): return lax.ppermute(value, AXES, pairs)]
  transfers between devices with their start and end apart: 4 -> 26, of which waited for: 4 -> 18; matrix products, arithmetic and copies ran while one was open for 23% -> 3% of each run, Pallas kernels for 0% -> 15%
where the time goes in v1:
time: 218 us; the launch traced here: 217 us
  waiting for transfers between devices  110 us (50%)
  Pallas kernels  62.7 us (29%)
  starting transfers between devices  30.1 us (14%)
  other arithmetic  7 us (3%)
  local copies, waits for them, and re-layouts  5.5 us (3%)
    ppermute x26, waiting for transfers between devices, permute(): return lax.ppermute(value, AXES, pairs)  110 us
    pallas_call x1, Pallas kernels, update(): pl.pallas_call(update_body, out_shape=[jax.ShapeDtypeStruct(work.shape, F...  30.4 us
    ppermute x26, starting transfers between devices, permute(): return lax.ppermute(value, AXES, pairs)  30.1 us
    pallas_call x1, Pallas kernels, solve(): pl.pallas_call(solve_body, out_shape=jax.ShapeDtypeStruct((PANELS, PANEL,...  15.1 us
    pallas_call x1, Pallas kernels, prep(): pl.pallas_call(prep_body, out_shape=[big, big, small, small], in_specs=[p...  11.6 us
  transfers between devices with their start and end apart: 26, of which 18 were waited for; matrix products, arithmetic and copies ran while one was open for 3% of the time, Pallas kernels for 15%

profile of v1, /device:TPU:0, one launch (start us, length us, event | category | flops | bytes accessed | tf_op | source)
XLA Modules:
  0.0 216.6 jit_solution(4585809439379330335)
XLA Ops:
  0.6 1.8 slice_bitcast_fusion
  2.5 1.3 slice_select_fusion.1
  5.2 1.6 collective-permute-done
  7.7 2.1 collective-permute-start.1
  9.8 3.8 %collective-permute-done.1 = f32[2,32,512]{2,1,0:T(8,128)S(1)} collective-permute-done((f32[2,32,512]{2,1,0:T(8,128)S(1)}, f32[2,32,512]{2,1,0:T(8,128)S(1)}, u32[]{:S(2)}, u32[]{:S(2)}) %collective-permute-start.1) | collective-permute-done | bytes 131104 | tf_op jit(solution)/shard_map/ppermute | solution.py:33
  14.6 3.9 %collective-permute-start.2 = (f32[3,32,512]{2,1,0:T(8,128)S(1)}, f32[3,32,512]{2,1,0:T(8,128)S(1)}, u32[]{:S(2)}, u32[]{:S(2)}) collective-permute-start(f32[3,32,512]{2,1,0:T(8,128)S(1)} %maximum_select_fusion), channel_id=1, source_target_pairs={{0,96},{1,97},{2,98},{3,99},{4,100},{5,101},{6,102},{7,103},{8,104... | collective-permute-start | bytes 589832 | tf_op jit(solution)/shard_map/ppermute | solution.py:33
  18.6 1.3 broadcast_select_fusion.1
  19.9 4.0 %collective-permute-done.2 = f32[3,32,512]{2,1,0:T(8,128)S(1)} collective-permute-done((f32[3,32,512]{2,1,0:T(8,128)S(1)}, f32[3,32,512]{2,1,0:T(8,128)S(1)}, u32[]{:S(2)}, u32[]{:S(2)}) %collective-permute-start.2) | collective-permute-done | bytes 196640 | tf_op jit(solution)/shard_map/ppermute | solution.py:33
  23.9 3.1 %collective-permute-start.5 = (f32[1,3,32,512]{3,2,1,0:T(8,128)S(1)}, f32[1,3,32,512]{3,2,1,0:T(8,128)S(1)}, u32[]{:S(2)}, u32[]{:S(2)}) collective-permute-start(f32[1,3,32,512]{3,2,1,0:T(8,128)S(1)} %select_bitcast_fusion.refs_0_), channel_id=1, source_target_pairs={{0,8},{1,9},{2,10},{3,11},{4,12},{5,13},{6,14},{7,15},{8,0},{9,1},... | collective-permute-start | bytes 589832 | tf_op jit(solution)/shard_map/ppermute | solution.py:33
  29.0 2.1 collective-permute-done.5.refs_3_
  31.1 2.2 %collective-permute-done.4.refs_2_ = f32[1,3,32,512]{3,2,1,0:T(8,128)S(1)} collective-permute-done((f32[1,3,32,512]{3,2,1,0:T(8,128)S(1)}, f32[1,3,32,512]{3,2,1,0:T(8,128)S(1)}, u32[]{:S(2)}, u32[]{:S(2)}) %collective-permute-start.4) | collective-permute-done | bytes 196640 | tf_op jit(solution)/shard_map/ppermute | solution.py:33
  33.3 1.7 collective-permute-done.3.refs_1_
  36.0 3.3 %collective-permute-start.8 = (f32[4,3,32,512]{3,2,1,0:T(8,128)S(1)}, f32[4,3,32,512]{3,2,1,0:T(8,128)S(1)}, u32[]{:S(2)}, u32[]{:S(2)}) collective-permute-start(f32[4,3,32,512]{3,2,1,0:T(8,128)S(1)} %shard_map.77.refs_0_), channel_id=1, source_target_pairs={{0,2},{1,3},{2,0},{3,1},{4,6},{5,7},{6,4},{7,5},{8,10},{9,11},{10,... | collective-permute-start | bytes 2359304 | tf_op jit(solution)/shard_map/ppermute | solution.py:33
  42.3 7.4 %collective-permute-done.8.refs_3_ = f32[4,3,32,512]{3,2,1,0:T(8,128)S(1)} collective-permute-done((f32[4,3,32,512]{3,2,1,0:T(8,128)S(1)}, f32[4,3,32,512]{3,2,1,0:T(8,128)S(1)}, u32[]{:S(2)}, u32[]{:S(2)}) %collective-permute-start.8) | collective-permute-done | bytes 786464 | tf_op jit(solution)/shard_map/ppermute | solution.py:33
  49.7 8.7 %collective-permute-done.7.refs_2_ = f32[4,3,32,512]{3,2,1,0:T(8,128)S(1)} collective-permute-done((f32[4,3,32,512]{3,2,1,0:T(8,128)S(1)}, f32[4,3,32,512]{3,2,1,0:T(8,128)S(1)}, u32[]{:S(2)}, u32[]{:S(2)}) %collective-permute-start.7) | collective-permute-done | bytes 786464 | tf_op jit(solution)/shard_map/ppermute | solution.py:33
  58.4 3.7 %pack.1.own = f32[3,512,512]{2,1,0:T(8,128)} custom-call(s32[20]{0:T(128)S(1)} %pad_add_fusion.1.tab, f32[4,3,32,512]{3,2,1,0:T(8,128)S(1)} %shard_map.77.refs_0_, f32[4,3,32,512]{3,2,1,0:T(8,128)S(1)} %collective-permute-done.6.refs_1_, f32[4,3,32,512]{3,2,1,0:T(8,128)S(1)} %collective-permute-done.7.refs_2_, ...), custom_call_target="tpu_custom_call" | custom-call | bytes 6291456 | tf_op jit(solution)/shard_map/pack/pallas_call | solution.py:132
  62.2 1.5 select_select_fusion
  63.7 1.3 collective-permute-start.12
  65.0 25.9 %collective-permute-done.12.r2 = f32[512,512]{1,0:T(8,128)S(1)} collective-permute-done((f32[512,512]{1,0:T(8,128)}, f32[512,512]{1,0:T(8,128)S(1)}, u32[]{:S(2)}, u32[]{:S(2)}) %collective-permute-start.12) | collective-permute-done | bytes 1048608 | tf_op jit(solution)/shard_map/ppermute | solution.py:33
  92.9 6.8 %collective-permute-done.17.refs_3_ = f32[1,2,3,32,512]{4,3,2,1,0:T(8,128)S(1)} collective-permute-done((f32[1,2,3,32,512]{4,3,2,1,0:T(8,128)S(1)}, f32[1,2,3,32,512]{4,3,2,1,0:T(8,128)S(1)}, u32[]{:S(2)}, u32[]{:S(2)}) %collective-permute-start.17) | collective-permute-done | bytes 393248 | tf_op jit(solution)/shard_map/ppermute | solution.py:33
  101.5 2.1 collective-permute-start.19
  103.6 3.6 %collective-permute-done.13.r3 = f32[512,512]{1,0:T(8,128)S(1)} collective-permute-done((f32[512,512]{1,0:T(8,128)S(1)}, f32[512,512]{1,0:T(8,128)S(1)}, u32[]{:S(2)}, u32[]{:S(2)}) %collective-permute-start.13) | collective-permute-done | bytes 1048608 | tf_op jit(solution)/shard_map/ppermute | solution.py:33
  107.2 7.5 %collective-permute-done.18.refs_1_ = f32[2,2,3,32,512]{4,3,2,1,0:T(8,128)S(1)} collective-permute-done((f32[2,2,3,32,512]{4,3,2,1,0:T(8,128)S(1)}, f32[2,2,3,32,512]{4,3,2,1,0:T(8,128)S(1)}, u32[]{:S(2)}, u32[]{:S(2)}) %collective-permute-start.18) | collective-permute-done | bytes 786464 | tf_op jit(solution)/shard_map/ppermute | solution.py:33
  116.1 11.6 %prep.1 = (bf16[6,512,512]{2,1,0:T(8,128)(2,1)}, bf16[6,512,512]{2,1,0:T(8,128)(2,1)}, bf16[3,4,128,128]{3,2,1,0:T(8,128)(2,1)}, bf16[3,4,128,128]{3,2,1,0:T(8,128)(2,1)}) custom-call(s32[20]{0:T(128)} %copy-done, f32[3,512]{1,0:T(4,128)} %piv.1, f32[3,512,512]{2,1,0:T(8,128)} %pack.1.own, f32[3,512,512]{2,1,0:T(8,128)} %collective-permute-done.9.other), custom_call_target="tpu_custom_call" | custom-call | flops 4294967296 | bytes 14680064 | tf_op jit(solution)/shard_map/prep/pallas_call | solution.py:210
  127.7 15.1 %solve.1.xa_hbm = f32[3,512,512]{2,1,0:T(8,128)} custom-call(s32[20]{0:T(128)} %copy-done, bf16[6,512,512]{2,1,0:T(8,128)(2,1)} %get-tuple-element.12.lh_h, bf16[6,512,512]{2,1,0:T(8,128)(2,1)} %get-tuple-element.13.ll_h, bf16[3,4,128,128]{3,2,1,0:T(8,128)(2,1)} %get-tuple-element.14.vh_h, bf16[3,4,128,128]{3,2,1,0:T(8,128)(2,1)} %get-tuple-element.15.vl_h, ...), custom_call_target="tpu_custom_call" | custom-call | flops 8589934592 | bytes 14680064 | tf_op jit(solution)/shard_map/solve/pallas_call | solution.py:284
  143.8 2.6 %collective-permute-start.21 = (f32[4,2,3,32,512]{4,3,2,1,0:T(8,128)S(1)}, f32[4,2,3,32,512]{4,3,2,1,0:T(8,128)S(1)}, u32[]{:S(2)}, u32[]{:S(2)}) collective-permute-start(f32[4,2,3,32,512]{4,3,2,1,0:T(8,128)S(1)} %get-tuple-element.18.refs_0_), channel_id=1, source_target_pairs={{0,3},{1,2},{2,1},{3,0},{4,7},{5,6},{6,5},{7,4},{8,11},{9,10},{10,... | collective-permute-start | bytes 4718600 | tf_op jit(solution)/shard_map/ppermute | solution.py:33
  146.4 3.0 %collective-permute-start.24 = (f32[4,2,3,32,512]{4,3,2,1,0:T(8,128)S(1)}, f32[4,2,3,32,512]{4,3,2,1,0:T(8,128)S(1)}, u32[]{:S(2)}, u32[]{:S(2)}) collective-permute-start(f32[4,2,3,32,512]{4,3,2,1,0:T(8,128)S(1)} %get-tuple-element.19.refs_4_), channel_id=1, source_target_pairs={{0,12},{1,13},{2,14},{3,15},{4,8},{5,9},{6,10},{7,11},{8,4},{9,5},... | collective-permute-start | bytes 4718600 | tf_op jit(solution)/shard_map/ppermute | solution.py:33
  151.0 14.4 %collective-permute-done.21.refs_2_ = f32[4,2,3,32,512]{4,3,2,1,0:T(8,128)S(1)} collective-permute-done((f32[4,2,3,32,512]{4,3,2,1,0:T(8,128)S(1)}, f32[4,2,3,32,512]{4,3,2,1,0:T(8,128)S(1)}, u32[]{:S(2)}, u32[]{:S(2)}) %collective-permute-start.21) | collective-permute-done | bytes 1572896 | tf_op jit(solution)/shard_map/ppermute | solution.py:33
  165.4 2.6 %collective-permute-done.24.refs_6_ = f32[4,2,3,32,512]{4,3,2,1,0:T(8,128)S(1)} collective-permute-done((f32[4,2,3,32,512]{4,3,2,1,0:T(8,128)S(1)}, f32[4,2,3,32,512]{4,3,2,1,0:T(8,128)S(1)}, u32[]{:S(2)}, u32[]{:S(2)}) %collective-permute-start.24) | collective-permute-done | bytes 1572896 | tf_op jit(solution)/shard_map/ppermute | solution.py:33
  168.0 14.3 %collective-permute-done.22.refs_3_ = f32[4,2,3,32,512]{4,3,2,1,0:T(8,128)S(1)} collective-permute-done((f32[4,2,3,32,512]{4,3,2,1,0:T(8,128)S(1)}, f32[4,2,3,32,512]{4,3,2,1,0:T(8,128)S(1)}, u32[]{:S(2)}, u32[]{:S(2)}) %collective-permute-start.22) | collective-permute-done | bytes 1572896 | tf_op jit(solution)/shard_map/ppermute | solution.py:33
  182.3 2.6 %collective-permute-done.25.refs_7_ = f32[4,2,3,32,512]{4,3,2,1,0:T(8,128)S(1)} collective-permute-done((f32[4,2,3,32,512]{4,3,2,1,0:T(8,128)S(1)}, f32[4,2,3,32,512]{4,3,2,1,0:T(8,128)S(1)}, u32[]{:S(2)}, u32[]{:S(2)}) %collective-permute-start.25) | collective-permute-done | bytes 1572896 | tf_op jit(solution)/shard_map/ppermute | solution.py:33
  186.0 30.4 %update.1 = (f32[4,512,1024]{2,1,0:T(8,128)}, f32[3,512,1024]{2,1,0:T(8,128)}) custom-call(s32[34]{0:T(128)} %pad_add_fusion.tab_ref, f32[3,512,512]{2,1,0:T(8,128)} %solve.1.xa_hbm, f32[3,512,512]{2,1,0:T(8,128)} %collective-permute-done.15.xb_hbm, f32[4,2,3,32,512]{4,3,2,1,0:T(8,128)} %copy-done.1, f32[4,2,3,32,512]{4,3,2,1,0:T(8,128)} %copy-done.11, ...), custom_call_target="tpu_custom_call" | custom-call | flops 21474836480 | bytes 44040192 | tf_op jit(solution)/shard_map/update/pallas_call | solution.py:373
  (83 shorter events, 18.3 us)
Async XLA Ops:
  3.8 14.7 %collective-permute-start.10 = (f32[512,512]{1,0:T(8,128)}, f32[512,512]{1,0:T(8,128)S(1)}, u32[]{:S(2)}, u32[]{:S(2)}) collective-permute-start(f32[512,512]{1,0:T(8,128)} %slice_select_fusion.1), channel_id=1, source_target_pairs={{0,16},{1,17},{2,18},{3,19},{4,20},{5,21},{6,22},{7,23},{8,24},{9,... | collective-permute-start | bytes 3145736 | tf_op jit(solution)/shard_map/ppermute | solution.py:33
  4.7 2.1 collective-permute-start
  7.7 5.9 %collective-permute-start.1 = (f32[2,32,512]{2,1,0:T(8,128)S(1)}, f32[2,32,512]{2,1,0:T(8,128)S(1)}, u32[]{:S(2)}, u32[]{:S(2)}) collective-permute-start(f32[2,32,512]{2,1,0:T(8,128)S(1)} %bitcast_select_fusion), channel_id=1, source_target_pairs={{0,32},{1,33},{2,34},{3,35},{4,36},{5,37},{6,38},{7,39},{8,40},{9,... | collective-permute-start | bytes 393224 | tf_op jit(solution)/shard_map/ppermute | solution.py:33
  14.6 9.2 %collective-permute-start.2 = (f32[3,32,512]{2,1,0:T(8,128)S(1)}, f32[3,32,512]{2,1,0:T(8,128)S(1)}, u32[]{:S(2)}, u32[]{:S(2)}) collective-permute-start(f32[3,32,512]{2,1,0:T(8,128)S(1)} %maximum_select_fusion), channel_id=1, source_target_pairs={{0,96},{1,97},{2,98},{3,99},{4,100},{5,101},{6,102},{7,103},{8,104... | collective-permute-start | bytes 589832 | tf_op jit(solution)/shard_map/ppermute | solution.py:33
  19.9 42.3 %collective-permute-start.11 = (f32[512,512]{1,0:T(8,128)}, f32[512,512]{1,0:T(8,128)}, u32[]{:S(2)}, u32[]{:S(2)}) collective-permute-start(f32[512,512]{1,0:T(8,128)} %broadcast_select_fusion.1), channel_id=1, source_target_pairs={{0,32},{1,33},{2,34},{3,35},{4,36},{5,37},{6,38},{7,39},{8,40},{9,... | collective-permute-start | bytes 3145736 | tf_op jit(solution)/shard_map/ppermute | solution.py:33
  23.9 7.3 %collective-permute-start.5 = (f32[1,3,32,512]{3,2,1,0:T(8,128)S(1)}, f32[1,3,32,512]{3,2,1,0:T(8,128)S(1)}, u32[]{:S(2)}, u32[]{:S(2)}) collective-permute-start(f32[1,3,32,512]{3,2,1,0:T(8,128)S(1)} %select_bitcast_fusion.refs_0_), channel_id=1, source_target_pairs={{0,8},{1,9},{2,10},{3,11},{4,12},{5,13},{6,14},{7,15},{8,0},{9,1},... | collective-permute-start | bytes 589832 | tf_op jit(solution)/shard_map/ppermute | solution.py:33
  27.0 6.3 %collective-permute-start.4 = (f32[1,3,32,512]{3,2,1,0:T(8,128)S(1)}, f32[1,3,32,512]{3,2,1,0:T(8,128)S(1)}, u32[]{:S(2)}, u32[]{:S(2)}) collective-permute-start(f32[1,3,32,512]{3,2,1,0:T(8,128)S(1)} %select_bitcast_fusion.refs_0_), channel_id=1, source_target_pairs={{0,12},{1,13},{2,14},{3,15},{4,0},{5,1},{6,2},{7,3},{8,4},{9,5},{1... | collective-permute-start | bytes 589832 | tf_op jit(solution)/shard_map/ppermute | solution.py:33
  28.1 6.9 %collective-permute-start.3 = (f32[1,3,32,512]{3,2,1,0:T(8,128)S(1)}, f32[1,3,32,512]{3,2,1,0:T(8,128)S(1)}, u32[]{:S(2)}, u32[]{:S(2)}) collective-permute-start(f32[1,3,32,512]{3,2,1,0:T(8,128)S(1)} %select_bitcast_fusion.refs_0_), channel_id=1, source_target_pairs={{0,4},{1,5},{2,6},{3,7},{4,8},{5,9},{6,10},{7,11},{8,12},{9,13},{1... | collective-permute-start | bytes 589832 | tf_op jit(solution)/shard_map/ppermute | solution.py:33
  36.0 13.7 %collective-permute-start.8 = (f32[4,3,32,512]{3,2,1,0:T(8,128)S(1)}, f32[4,3,32,512]{3,2,1,0:T(8,128)S(1)}, u32[]{:S(2)}, u32[]{:S(2)}) collective-permute-start(f32[4,3,32,512]{3,2,1,0:T(8,128)S(1)} %shard_map.77.refs_0_), channel_id=1, source_target_pairs={{0,2},{1,3},{2,0},{3,1},{4,6},{5,7},{6,4},{7,5},{8,10},{9,11},{10,... | collective-permute-start | bytes 2359304 | tf_op jit(solution)/shard_map/ppermute | solution.py:33
  39.3 19.1 %collective-permute-start.7 = (f32[4,3,32,512]{3,2,1,0:T(8,128)S(1)}, f32[4,3,32,512]{3,2,1,0:T(8,128)S(1)}, u32[]{:S(2)}, u32[]{:S(2)}) collective-permute-start(f32[4,3,32,512]{3,2,1,0:T(8,128)S(1)} %shard_map.77.refs_0_), channel_id=1, source_target_pairs={{0,3},{1,0},{2,1},{3,2},{4,7},{5,4},{6,5},{7,6},{8,11},{9,8},{10,9... | collective-permute-start | bytes 2359304 | tf_op jit(solution)/shard_map/ppermute | solution.py:33
  40.3 18.1 %collective-permute-start.6 = (f32[4,3,32,512]{3,2,1,0:T(8,128)S(1)}, f32[4,3,32,512]{3,2,1,0:T(8,128)S(1)}, u32[]{:S(2)}, u32[]{:S(2)}) collective-permute-start(f32[4,3,32,512]{3,2,1,0:T(8,128)S(1)} %shard_map.77.refs_0_), channel_id=1, source_target_pairs={{0,1},{1,2},{2,3},{3,0},{4,5},{5,6},{6,7},{7,4},{8,9},{9,10},{10,1... | collective-permute-start | bytes 2359304 | tf_op jit(solution)/shard_map/ppermute | solution.py:33
  62.1 54.0 %collective-permute-start.9 = (f32[3,512,512]{2,1,0:T(8,128)}, f32[3,512,512]{2,1,0:T(8,128)}, u32[]{:S(2)}, u32[]{:S(2)}) collective-permute-start(f32[3,512,512]{2,1,0:T(8,128)} %pack.1.own), channel_id=1, source_target_pairs={{0,16},{1,17},{2,18},{3,19},{4,20},{5,21},{6,22},{7,23},{8,24},{9,... | collective-permute-start | bytes 9437192 | tf_op jit(solution)/shard_map/ppermute | solution.py:33
  63.7 27.5 %copy-start.7 = (f32[4,3,32,512]{3,2,1,0:T(8,128)S(1)}, f32[4,3,32,512]{3,2,1,0:T(8,128)}, u32[]{:S(2)}) copy-start(f32[4,3,32,512]{3,2,1,0:T(8,128)} %param.6) | copy-start | bytes 2359300
  63.7 27.2 %collective-permute-start.12 = (f32[512,512]{1,0:T(8,128)}, f32[512,512]{1,0:T(8,128)S(1)}, u32[]{:S(2)}, u32[]{:S(2)}) collective-permute-start(f32[512,512]{1,0:T(8,128)} %select_select_fusion), channel_id=1, source_target_pairs={{0,32},{1,33},{2,34},{3,35},{4,36},{5,37},{6,38},{7,39},{8,40},{9,... | collective-permute-start | bytes 3145736 | tf_op jit(solution)/shard_map/ppermute | solution.py:33
  91.1 16.1 %collective-permute-start.13 = (f32[512,512]{1,0:T(8,128)S(1)}, f32[512,512]{1,0:T(8,128)S(1)}, u32[]{:S(2)}, u32[]{:S(2)}) collective-permute-start(f32[512,512]{1,0:T(8,128)S(1)} %broadcast_select_fusion), channel_id=1, source_target_pairs={{0,32},{1,33},{2,34},{3,35},{4,36},{5,37},{6,38},{7,39},{8,40},{9,... | collective-permute-start | bytes 3145736 | tf_op jit(solution)/shard_map/ppermute | solution.py:33
  91.9 7.8 %collective-permute-start.17 = (f32[1,2,3,32,512]{4,3,2,1,0:T(8,128)S(1)}, f32[1,2,3,32,512]{4,3,2,1,0:T(8,128)S(1)}, u32[]{:S(2)}, u32[]{:S(2)}) collective-permute-start(f32[1,2,3,32,512]{4,3,2,1,0:T(8,128)S(1)} %get-tuple-element.22.refs_2_), channel_id=1, source_target_pairs={{0,1},{1,0},{2,3},{3,2},{4,5},{5,4},{6,7},{7,6},{8,9},{9,8},{10,11... | collective-permute-start | bytes 1179656 | tf_op jit(solution)/shard_map/ppermute | solution.py:33
  92.9 7.8 %collective-permute-start.16 = (f32[1,2,3,32,512]{4,3,2,1,0:T(8,128)S(1)}, f32[1,2,3,32,512]{4,3,2,1,0:T(8,128)S(1)}, u32[]{:S(2)}, u32[]{:S(2)}) collective-permute-start(f32[1,2,3,32,512]{4,3,2,1,0:T(8,128)S(1)} %get-tuple-element.23.refs_0_), channel_id=1, source_target_pairs={{0,4},{1,5},{2,6},{3,7},{4,0},{5,1},{6,2},{7,3},{8,12},{9,13},{10,... | collective-permute-start | bytes 1179656 | tf_op jit(solution)/shard_map/ppermute | solution.py:33
  101.4 13.3 %collective-permute-start.18 = (f32[2,2,3,32,512]{4,3,2,1,0:T(8,128)S(1)}, f32[2,2,3,32,512]{4,3,2,1,0:T(8,128)S(1)}, u32[]{:S(2)}, u32[]{:S(2)}) collective-permute-start(f32[2,2,3,32,512]{4,3,2,1,0:T(8,128)S(1)} %get-tuple-element.16.refs_0_), channel_id=1, source_target_pairs={{0,12},{1,13},{2,14},{3,15},{4,8},{5,9},{6,10},{7,11},{8,4},{9,5},... | collective-permute-start | bytes 2359304 | tf_op jit(solution)/shard_map/ppermute | solution.py:33
  101.5 13.3 %collective-permute-start.19 = (f32[2,2,3,32,512]{4,3,2,1,0:T(8,128)S(1)}, f32[2,2,3,32,512]{4,3,2,1,0:T(8,128)S(1)}, u32[]{:S(2)}, u32[]{:S(2)}) collective-permute-start(f32[2,2,3,32,512]{4,3,2,1,0:T(8,128)S(1)} %get-tuple-element.17.refs_2_), channel_id=1, source_target_pairs={{0,3},{1,2},{2,1},{3,0},{4,7},{5,6},{6,5},{7,4},{8,11},{9,10},{10,... | collective-permute-start | bytes 2359304 | tf_op jit(solution)/shard_map/ppermute | solution.py:33
  107.2 20.5 %collective-permute-start.14 = (f32[512,512]{1,0:T(8,128)S(1)}, f32[512,512]{1,0:T(8,128)}, u32[]{:S(2)}, u32[]{:S(2)}) collective-permute-start(f32[512,512]{1,0:T(8,128)S(1)} %collective-permute-done.13.r3), channel_id=1, source_target_pairs={{0,32},{1,33},{2,34},{3,35},{4,36},{5,37},{6,38},{7,39},{8,40},{9,... | collective-permute-start | bytes 3145736 | tf_op jit(solution)/shard_map/ppermute | solution.py:33
  115.0 28.8 %copy-start.1 = (f32[4,2,3,32,512]{4,3,2,1,0:T(8,128)}, f32[4,2,3,32,512]{4,3,2,1,0:T(8,128)S(1)}, u32[]{:S(2)}) copy-start(f32[4,2,3,32,512]{4,3,2,1,0:T(8,128)S(1)} %get-tuple-element.18.refs_0_) | copy-start | bytes 4718596
  115.0 31.4 %copy-start.2 = (f32[4,2,3,32,512]{4,3,2,1,0:T(8,128)}, f32[4,2,3,32,512]{4,3,2,1,0:T(8,128)S(1)}, u32[]{:S(2)}) copy-start(f32[4,2,3,32,512]{4,3,2,1,0:T(8,128)S(1)} %get-tuple-element.19.refs_4_) | copy-start | bytes 4718596
  115.0 34.3 %collective-permute-start.20 = (f32[4,2,3,32,512]{4,3,2,1,0:T(8,128)S(1)}, f32[4,2,3,32,512]{4,3,2,1,0:T(8,128)S(1)}, u32[]{:S(2)}, u32[]{:S(2)}) collective-permute-start(f32[4,2,3,32,512]{4,3,2,1,0:T(8,128)S(1)} %get-tuple-element.18.refs_0_), channel_id=1, source_target_pairs={{0,1},{1,0},{2,3},{3,2},{4,5},{5,4},{6,7},{7,6},{8,9},{9,8},{10,11... | collective-permute-start | bytes 4718600 | tf_op jit(solution)/shard_map/ppermute | solution.py:33
  116.1 33.9 %collective-permute-start.23 = (f32[4,2,3,32,512]{4,3,2,1,0:T(8,128)S(1)}, f32[4,2,3,32,512]{4,3,2,1,0:T(8,128)S(1)}, u32[]{:S(2)}, u32[]{:S(2)}) collective-permute-start(f32[4,2,3,32,512]{4,3,2,1,0:T(8,128)S(1)} %get-tuple-element.19.refs_4_), channel_id=1, source_target_pairs={{0,4},{1,5},{2,6},{3,7},{4,0},{5,1},{6,2},{7,3},{8,12},{9,13},{10,... | collective-permute-start | bytes 4718600 | tf_op jit(solution)/shard_map/ppermute | solution.py:33
  127.7 22.6 %copy-start.9 = (s32[32]{0:T(128)S(1)}, s32[32]{0:T(128)}, u32[]{:S(2)}) copy-start(s32[32]{0:T(128)} %constant.206.clone) | copy-start | bytes 388
  127.7 22.6 %copy-start.10 = (s32[32]{0:T(128)S(1)}, s32[32]{0:T(128)}, u32[]{:S(2)}) copy-start(s32[32]{0:T(128)} %constant.205.clone) | copy-start | bytes 388
  142.8 43.2 %collective-permute-start.15 = (f32[3,512,512]{2,1,0:T(8,128)}, f32[3,512,512]{2,1,0:T(8,128)}, u32[]{:S(2)}, u32[]{:S(2)}) collective-permute-start(f32[3,512,512]{2,1,0:T(8,128)} %solve.1.xa_hbm), channel_id=1, source_target_pairs={{0,16},{1,17},{2,18},{3,19},{4,20},{5,21},{6,22},{7,23},{8,24},{9,... | collective-permute-start | bytes 9437192 | tf_op jit(solution)/shard_map/ppermute | solution.py:33
  143.8 21.6 %collective-permute-start.21 = (f32[4,2,3,32,512]{4,3,2,1,0:T(8,128)S(1)}, f32[4,2,3,32,512]{4,3,2,1,0:T(8,128)S(1)}, u32[]{:S(2)}, u32[]{:S(2)}) collective-permute-start(f32[4,2,3,32,512]{4,3,2,1,0:T(8,128)S(1)} %get-tuple-element.18.refs_0_), channel_id=1, source_target_pairs={{0,3},{1,2},{2,1},{3,0},{4,7},{5,6},{6,5},{7,4},{8,11},{9,10},{10,... | collective-permute-start | bytes 4718600 | tf_op jit(solution)/shard_map/ppermute | solution.py:33
  146.4 21.6 %collective-permute-start.24 = (f32[4,2,3,32,512]{4,3,2,1,0:T(8,128)S(1)}, f32[4,2,3,32,512]{4,3,2,1,0:T(8,128)S(1)}, u32[]{:S(2)}, u32[]{:S(2)}) collective-permute-start(f32[4,2,3,32,512]{4,3,2,1,0:T(8,128)S(1)} %get-tuple-element.19.refs_4_), channel_id=1, source_target_pairs={{0,12},{1,13},{2,14},{3,15},{4,8},{5,9},{6,10},{7,11},{8,4},{9,5},... | collective-permute-start | bytes 4718600 | tf_op jit(solution)/shard_map/ppermute | solution.py:33
  149.3 32.9 %collective-permute-start.22 = (f32[4,2,3,32,512]{4,3,2,1,0:T(8,128)S(1)}, f32[4,2,3,32,512]{4,3,2,1,0:T(8,128)S(1)}, u32[]{:S(2)}, u32[]{:S(2)}) collective-permute-start(f32[4,2,3,32,512]{4,3,2,1,0:T(8,128)S(1)} %collective-permute-done.20.refs_1_), channel_id=1, source_target_pairs={{0,3},{1,2},{2,1},{3,0},{4,7},{5,6},{6,5},{7,4},{8,11},{9,10},{10,... | collective-permute-start | bytes 4718600 | tf_op jit(solution)/shard_map/ppermute | solution.py:33
  149.9 32.3 %copy-start.12 = (f32[4,2,3,32,512]{4,3,2,1,0:T(8,128)}, f32[4,2,3,32,512]{4,3,2,1,0:T(8,128)S(1)}, u32[]{:S(2)}) copy-start(f32[4,2,3,32,512]{4,3,2,1,0:T(8,128)S(1)} %collective-permute-done.23.refs_5_) | copy-start | bytes 4718596
  149.9 34.9 %collective-permute-start.25 = (f32[4,2,3,32,512]{4,3,2,1,0:T(8,128)S(1)}, f32[4,2,3,32,512]{4,3,2,1,0:T(8,128)S(1)}, u32[]{:S(2)}, u32[]{:S(2)}) collective-permute-start(f32[4,2,3,32,512]{4,3,2,1,0:T(8,128)S(1)} %collective-permute-done.23.refs_5_), channel_id=1, source_target_pairs={{0,12},{1,13},{2,14},{3,15},{4,8},{5,9},{6,10},{7,11},{8,4},{9,5},... | collective-permute-start | bytes 4718600 | tf_op jit(solution)/shard_map/ppermute | solution.py:33
  (12 other events, 157.3 us)

commit v2 on v1

--- a/solution.py
+++ b/solution.py
@@ -220,7 +220,7 @@
             pltpu.VMEM((PANELS, 4, 128, 128), BF16),
             pltpu.SemaphoreType.DMA((6,)),
         ],
-        compiler_params=pltpu.CompilerParams(vmem_limit_bytes=56 << 20),
+        compiler_params=pltpu.CompilerParams(vmem_limit_bytes=28 << 20),
         cost_estimate=pl.CostEstimate(flops=4 << 30, bytes_accessed=14 << 20, transcendentals=0),
         name="prep",
     )(tab, pivots, own, other)
@@ -298,7 +298,7 @@
             pltpu.SemaphoreType.DMA,
             pltpu.SemaphoreType.DMA((PANELS,)),
         ],
-        compiler_params=pltpu.CompilerParams(vmem_limit_bytes=56 << 20),
+        compiler_params=pltpu.CompilerParams(vmem_limit_bytes=28 << 20),
         cost_estimate=pl.CostEstimate(flops=8 << 30, bytes_accessed=14 << 20, transcendentals=0),
         name="solve",
     )(tab, *factors, rhs, swp, *recvs)
@@ -311,9 +311,9 @@
     b = step // 2
     core = tab_ref[0]
     row = tab_ref[1]
-    xc = [pltpu.make_async_copy(src, xv.at[:, :, pl.ds(pl.multiple_of(h * HALF, HALF), HALF)], sem_x.at[k])
-          for k, (src, h) in enumerate(((xa_hbm, core), (xb_hbm, 1 - core)))]
-    out_copy = pltpu.make_async_copy(xv, solved, sem_x.at[2])
+    xc = [[pltpu.make_async_copy(src.at[p], xv.at[p, :, pl.ds(pl.multiple_of(h * HALF, HALF), HALF)], sem_x.at[p])
+           for src, h in ((xa_hbm, core), (xb_hbm, 1 - core))] for p in range(PANELS)]
+    out_copy = pltpu.make_async_copy(xv, solved, sem_x.at[PANELS])
 
     def fcopies(color, inner, slot):
         for q in range(4):
@@ -331,32 +331,41 @@
 
     slot = lax.rem(b, 2)
 
+    def panel(p, cols):
+        keep = jnp.logical_or(b > 0, row > p)
+        return jnp.where(keep, fv[slot, p, :, cols], 0.0)
+
     @pl.when(step == 0)
     def _():
-        for c in xc:
-            c.start()
         start(0, 0)
+        for p in range(PANELS):
+            for c in xc[p]:
+                c.start()
         start(1, 1)
-        for c in xc:
+        for c in fcopies(0, 0, 0):
             c.wait()
+        acc = work_ref[0]
+        for p in range(PANELS):
+            for c in xc[p]:
+                c.wait()
+            rows = slice(p * PANEL, p * PANEL + PANEL)
+            hi, lo = split(xv[p])
+            xh[rows, :] = hi
+            xl[rows, :] = lo
+            acc = acc - dot3(split(panel(p, slice(0, 256))), (hi, lo), TN)
         out_copy.start()
-        for p in range(PANELS):
-            hi, lo = split(xv[p])
-            xh[p * PANEL:p * PANEL + PANEL, :] = hi
-            xl[p * PANEL:p * PANEL + PANEL, :] = lo
-
-    @pl.when(lax.rem(step, 2) == 0)
+        out_ref[0] = acc
+
+    @pl.when((lax.rem(step, 2) == 0) & (step > 0))
     def _():
         for c in fcopies(0, 0, slot):
             c.wait()
 
-    cols = pl.ds(pl.multiple_of(lax.rem(step, 2) * 256, 256), 256)
-    fs = []
-    for p in range(PANELS):
-        keep = jnp.logical_or(b > 0, row > p)
-        fs.append(jnp.where(keep, fv[slot, p, :, cols], 0.0))
-    up = dot3(split(jnp.concatenate(fs, 0)), (xh[...], xl[...]), TN)
-    out_ref[0] = work_ref[0] - up
+    @pl.when(step > 0)
+    def _():
+        cols = pl.ds(pl.multiple_of(lax.rem(step, 2) * 256, 256), 256)
+        f = jnp.concatenate([panel(p, cols) for p in range(PANELS)], 0)
+        out_ref[0] = work_ref[0] - dot3(split(f), (xh[...], xl[...]), TN)
 
     @pl.when((lax.rem(step, 2) == 1) & (b + 2 < 4))
     def _():
@@ -382,11 +391,11 @@
                 pltpu.VMEM((PANELS * PANEL, NCOL), BF16),
                 pltpu.VMEM((PANELS * PANEL, NCOL), BF16),
                 pltpu.VMEM((2, PANELS, PANEL, PANEL), F32),
-                pltpu.SemaphoreType.DMA((3,)),
+                pltpu.SemaphoreType.DMA((PANELS + 1,)),
                 pltpu.SemaphoreType.DMA((2,)),
             ],
         ),
-        compiler_params=pltpu.CompilerParams(vmem_limit_bytes=60 << 20),
+        compiler_params=pltpu.CompilerParams(vmem_limit_bytes=54 << 20),
         cost_estimate=pl.CostEstimate(flops=20 << 30, bytes_accessed=42 << 20, transcendentals=0),
         name="update",
     )(tab, xa, xb, *bufs_a, *bufs_b, work)
@@ -412,19 +421,19 @@
     first = core == 0
 
     swl = swap_cores(factor[0, 2])
-    half_a, half_b = factor[0:2][None], factor[2:4][None]
-    ra1 = xor_wave(half_a, 0, 0)
     pay = factor[0, 0:2]
     pay = jnp.where((core == 1) & (z == 1), jnp.broadcast_to(swl[None], pay.shape), pay)
+    pay, later_factor, slab = lax.optimization_barrier((pay, factor, rhs))
     got = z_xor(pay, 1)
     low = jnp.where(z == 0, pay, got)
     high = jnp.where(z == 0, got, pay)
     share = jnp.where(first, jnp.stack([low[0], high[0], high[1]]), jnp.stack([low[0], low[1], high[0]]))
 
-    slab = rhs[0]
-    theirs = jnp.where(first, slab[:, HALF:], slab[:, :HALF])
-    mine = jnp.where(first, slab[:, :HALF], slab[:, HALF:])
+    theirs = lax.dynamic_slice(slab, (0, 0, (1 - core) * HALF), (1, PANEL, HALF))[0]
+    mine = lax.dynamic_slice(slab, (0, 0, core * HALF), (1, PANEL, HALF))[0]
     swp = swap_cores(theirs)
+    half_a, half_b = later_factor[0:2][None], later_factor[2:4][None]
+    ra1 = xor_wave(half_a, 0, 0)
     rb1 = xor_wave(half_b, 1, 0)
     share = jnp.where(z < 2, share, z_xor(share, 3))
 

time: 218 us -> 211 us (0.968)
  Pallas kernels: 62.7 us -> 55.1 us
    pallas_call x1, Pallas kernels: 15.1 us -> 10.7 us  [solve(): pl.pallas_call(solve_body, out_shape=jax.ShapeDtypeStruct((PANELS, PANEL,...]
    ppermute x26, waiting for transfers between devices: 110 us -> 108 us  [permute(): return lax.ppermute(value, AXES, pairs)]
  transfers between devices with their start and end apart: 26 -> 26, of which waited for: 18 -> 18; matrix products, arithmetic and copies ran while one was open for 3% -> 4% of each run, Pallas kernels for 15% -> 13%
where the time goes in v2:
time: 211 us; the launch traced here: 209 us
  waiting for transfers between devices  108 us (51%)
  Pallas kernels  55.1 us (26%)
  starting transfers between devices  29.2 us (14%)
  other arithmetic  8.05 us (4%)
  local copies, waits for them, and re-layouts  7.1 us (3%)
    ppermute x26, waiting for transfers between devices, permute(): return lax.ppermute(value, AXES, pairs)  108 us
    ppermute x26, starting transfers between devices, permute(): return lax.ppermute(value, AXES, pairs)  29.2 us
    pallas_call x1, Pallas kernels, update(): pl.pallas_call(update_body, out_shape=[jax.ShapeDtypeStruct(work.shape, F...  28.7 us
    pallas_call x1, Pallas kernels, solve(): pl.pallas_call(solve_body, out_shape=jax.ShapeDtypeStruct((PANELS, PANEL,...  10.7 us
    pallas_call x1, Pallas kernels, prep(): pl.pallas_call(prep_body, out_shape=[big, big, small, small], in_specs=[p...  9.46 us
    pallas_call x1, Pallas kernels, pack(): pl.pallas_call(pack_body, out_shape=jax.ShapeDtypeStruct((PANELS, PANEL,...  4.25 us
  transfers between devices with their start and end apart: 26, of which 18 were waited for; matrix products, arithmetic and copies ran while one was open for 4% of the time, Pallas kernels for 13%

profile of v2, /device:TPU:0, one launch (start us, length us, event | category | flops | bytes accessed | tf_op | source)
XLA Modules:
  0.0 208.6 jit_solution(6802230653898487038)
XLA Ops:
  5.2 2.0 collective-permute-start.1
  7.2 4.0 %collective-permute-done.1 = f32[2,32,512]{2,1,0:T(8,128)S(1)} collective-permute-done((f32[2,32,512]{2,1,0:T(8,128)S(1)}, f32[2,32,512]{2,1,0:T(8,128)S(1)}, u32[]{:S(2)}, u32[]{:S(2)}) %collective-permute-start.1) | collective-permute-done | bytes 131104 | tf_op jit(solution)/shard_map/ppermute | solution.py:33
  11.3 3.9 %collective-permute-start.2 = (f32[3,32,512]{2,1,0:T(8,128)S(1)}, f32[3,32,512]{2,1,0:T(8,128)S(1)}, u32[]{:S(2)}, u32[]{:S(2)}) collective-permute-start(f32[3,32,512]{2,1,0:T(8,128)S(1)} %maximum_select_fusion), channel_id=1, source_target_pairs={{0,96},{1,97},{2,98},{3,99},{4,100},{5,101},{6,102},{7,103},{8,104... | collective-permute-start | bytes 589832 | tf_op jit(solution)/shard_map/ppermute | solution.py:33
  15.3 2.4 %bitcast_select_fusion.1 = f32[512,512]{1,0:T(8,128)} fusion(f32[512,512]{1,0:T(8,128)S(1)} %collective-permute-done.10.swp, f32[4,512,1024]{2,1,0:T(8,128)} %refs_8_.1, s32[]{:T(128)S(6)} %select_n.275, pred[]{:T(512)S(6)} %eq.84), kind=kLoop, calls=%fused_computation.1 | loop fusion | flops 262144 | bytes 3145733 | tf_op jit(solution)/shard_map/jit(_where)/select_n | solution.py:440
  17.7 2.9 %collective-permute-done.2 = f32[3,32,512]{2,1,0:T(8,128)S(1)} collective-permute-done((f32[3,32,512]{2,1,0:T(8,128)S(1)}, f32[3,32,512]{2,1,0:T(8,128)S(1)}, u32[]{:S(2)}, u32[]{:S(2)}) %collective-permute-start.2) | collective-permute-done | bytes 196640 | tf_op jit(solution)/shard_map/ppermute | solution.py:33
  20.6 3.1 %collective-permute-start.5 = (f32[1,3,32,512]{3,2,1,0:T(8,128)S(1)}, f32[1,3,32,512]{3,2,1,0:T(8,128)S(1)}, u32[]{:S(2)}, u32[]{:S(2)}) collective-permute-start(f32[1,3,32,512]{3,2,1,0:T(8,128)S(1)} %select_bitcast_fusion.refs_0_), channel_id=1, source_target_pairs={{0,8},{1,9},{2,10},{3,11},{4,12},{5,13},{6,14},{7,15},{8,0},{9,1},... | collective-permute-start | bytes 589832 | tf_op jit(solution)/shard_map/ppermute | solution.py:33
  25.7 2.1 %collective-permute-done.5.refs_3_ = f32[1,3,32,512]{3,2,1,0:T(8,128)S(1)} collective-permute-done((f32[1,3,32,512]{3,2,1,0:T(8,128)S(1)}, f32[1,3,32,512]{3,2,1,0:T(8,128)S(1)}, u32[]{:S(2)}, u32[]{:S(2)}) %collective-permute-start.5) | collective-permute-done | bytes 196640 | tf_op jit(solution)/shard_map/ppermute | solution.py:33
  27.8 2.2 %collective-permute-done.4.refs_2_ = f32[1,3,32,512]{3,2,1,0:T(8,128)S(1)} collective-permute-done((f32[1,3,32,512]{3,2,1,0:T(8,128)S(1)}, f32[1,3,32,512]{3,2,1,0:T(8,128)S(1)}, u32[]{:S(2)}, u32[]{:S(2)}) %collective-permute-start.4) | collective-permute-done | bytes 196640 | tf_op jit(solution)/shard_map/ppermute | solution.py:33
  30.0 1.7 collective-permute-done.3.refs_1_
  32.7 3.3 %collective-permute-start.8 = (f32[4,3,32,512]{3,2,1,0:T(8,128)S(1)}, f32[4,3,32,512]{3,2,1,0:T(8,128)}, u32[]{:S(2)}, u32[]{:S(2)}) collective-permute-start(f32[4,3,32,512]{3,2,1,0:T(8,128)S(1)} %shard_map.77.refs_0_), channel_id=1, source_target_pairs={{0,2},{1,3},{2,0},{3,1},{4,6},{5,7},{6,4},{7,5},{8,10},{9,11},{10,... | collective-permute-start | bytes 2359304 | tf_op jit(solution)/shard_map/ppermute | solution.py:33
  39.0 7.5 %collective-permute-done.8.refs_3_ = f32[4,3,32,512]{3,2,1,0:T(8,128)} collective-permute-done((f32[4,3,32,512]{3,2,1,0:T(8,128)S(1)}, f32[4,3,32,512]{3,2,1,0:T(8,128)}, u32[]{:S(2)}, u32[]{:S(2)}) %collective-permute-start.8) | collective-permute-done | bytes 786464 | tf_op jit(solution)/shard_map/ppermute | solution.py:33
  46.5 8.7 %collective-permute-done.7.refs_2_ = f32[4,3,32,512]{3,2,1,0:T(8,128)} collective-permute-done((f32[4,3,32,512]{3,2,1,0:T(8,128)S(1)}, f32[4,3,32,512]{3,2,1,0:T(8,128)}, u32[]{:S(2)}, u32[]{:S(2)}) %collective-permute-start.7) | collective-permute-done | bytes 786464 | tf_op jit(solution)/shard_map/ppermute | solution.py:33
  55.2 4.3 %pack.1.own = f32[3,512,512]{2,1,0:T(8,128)} custom-call(s32[20]{0:T(128)S(1)} %pad_add_fusion.1.tab, f32[4,3,32,512]{3,2,1,0:T(8,128)S(1)} %shard_map.77.refs_0_, f32[4,3,32,512]{3,2,1,0:T(8,128)} %collective-permute-done.6.refs_1_, f32[4,3,32,512]{3,2,1,0:T(8,128)} %collective-permute-done.7.refs_2_, f32[4,3,32,512]{3,2,1,0:T(8,128)} %collective-permute-done.8.refs_3_), custom_call_target="tpu_custom_call" | custom-call | bytes 6291456 | tf_op jit(solution)/shard_map/pack/pallas_call | solution.py:132
  59.6 2.5 %fusion = f32[512,512]{1,0:T(8,128)} fusion(f32[512,512]{1,0:T(8,128)S(1)} %collective-permute-done.11.r1, f32[512,512]{1,0:T(8,128)S(1)} %collective-permute-done.10.swp, f32[4,512,1024]{2,1,0:T(8,128)} %refs_8_.1, s32[]{:T(128)S(6)} %select_n.275, pred[]{:T(512)S(6)} %eq.85, pred[]{:T(512)S(6)} %eq.84), kind=kLoop, calls=%fused_computation.2 | loop fusion | flops 524288 | bytes 4194310 | tf_op jit(solution)/shard_map/jit(_where)/select_n | solution.py:441
  62.1 25.4 %collective-permute-done.12.r2 = f32[512,512]{1,0:T(8,128)} collective-permute-done((f32[512,512]{1,0:T(8,128)}, f32[512,512]{1,0:T(8,128)}, u32[]{:S(2)}, u32[]{:S(2)}) %collective-permute-start.12) | collective-permute-done | bytes 1048608 | tf_op jit(solution)/shard_map/ppermute | solution.py:33
  87.5 1.4 broadcast_select_fusion
  90.2 1.4 collective-permute-start.17
  91.6 6.4 %collective-permute-done.17.refs_3_ = f32[1,2,3,32,512]{4,3,2,1,0:T(8,128)S(1)} collective-permute-done((f32[1,2,3,32,512]{4,3,2,1,0:T(8,128)S(1)}, f32[1,2,3,32,512]{4,3,2,1,0:T(8,128)S(1)}, u32[]{:S(2)}, u32[]{:S(2)}) %collective-permute-start.17) | collective-permute-done | bytes 393248 | tf_op jit(solution)/shard_map/ppermute | solution.py:33
  100.3 2.1 %collective-permute-start.19 = (f32[2,2,3,32,512]{4,3,2,1,0:T(8,128)S(1)}, f32[2,2,3,32,512]{4,3,2,1,0:T(8,128)S(1)}, u32[]{:S(2)}, u32[]{:S(2)}) collective-permute-start(f32[2,2,3,32,512]{4,3,2,1,0:T(8,128)S(1)} %get-tuple-element.23.refs_2_), channel_id=1, source_target_pairs={{0,3},{1,2},{2,1},{3,0},{4,7},{5,6},{6,5},{7,4},{8,11},{9,10},{10,... | collective-permute-start | bytes 2359304 | tf_op jit(solution)/shard_map/ppermute | solution.py:33
  102.4 2.6 %collective-permute-done.13.r3 = f32[512,512]{1,0:T(8,128)S(1)} collective-permute-done((f32[512,512]{1,0:T(8,128)S(1)}, f32[512,512]{1,0:T(8,128)S(1)}, u32[]{:S(2)}, u32[]{:S(2)}) %collective-permute-start.13) | collective-permute-done | bytes 1048608 | tf_op jit(solution)/shard_map/ppermute | solution.py:33
  105.0 8.4 %collective-permute-done.18.refs_1_ = f32[2,2,3,32,512]{4,3,2,1,0:T(8,128)S(1)} collective-permute-done((f32[2,2,3,32,512]{4,3,2,1,0:T(8,128)S(1)}, f32[2,2,3,32,512]{4,3,2,1,0:T(8,128)S(1)}, u32[]{:S(2)}, u32[]{:S(2)}) %collective-permute-start.18) | collective-permute-done | bytes 786464 | tf_op jit(solution)/shard_map/ppermute | solution.py:33
  114.5 9.5 %prep.1 = (bf16[6,512,512]{2,1,0:T(8,128)(2,1)S(1)}, bf16[6,512,512]{2,1,0:T(8,128)(2,1)S(1)}, bf16[3,4,128,128]{3,2,1,0:T(8,128)(2,1)S(1)}, bf16[3,4,128,128]{3,2,1,0:T(8,128)(2,1)S(1)}) custom-call(s32[20]{0:T(128)S(1)} %pad_add_fusion.1.tab, f32[3,512]{1,0:T(4,128)S(1)} %copy-done.3, f32[3,512,512]{2,1,0:T(8,128)} %pack.1.own, ...), custom_call_target="tpu_custom_call" | custom-call | flops 4294967296 | bytes 14680064 | tf_op jit(solution)/shard_map/prep/pallas_call | solution.py:210
  124.0 10.7 %solve.1.xa_hbm = f32[3,512,512]{2,1,0:T(8,128)S(1)} custom-call(s32[20]{0:T(128)S(1)} %pad_add_fusion.1.tab, bf16[6,512,512]{2,1,0:T(8,128)(2,1)S(1)} %get-tuple-element.16.lh_h, bf16[6,512,512]{2,1,0:T(8,128)(2,1)S(1)} %get-tuple-element.17.ll_h, bf16[3,4,128,128]{3,2,1,0:T(8,128)(2,1)S(1)} %get-tuple-element.18.vh_h, ...), custom_call_target="tpu_custom_call" | custom-call | flops 8589934592 | bytes 14680064 | tf_op jit(solution)/shard_map/solve/pallas_call | solution.py:284
  134.7 1.7 collective-permute-start.15
  136.4 1.9 collective-permute-start.21
  138.3 2.7 %collective-permute-start.24 = (f32[4,2,3,32,512]{4,3,2,1,0:T(8,128)S(1)}, f32[4,2,3,32,512]{4,3,2,1,0:T(8,128)S(1)}, u32[]{:S(2)}, u32[]{:S(2)}) collective-permute-start(f32[4,2,3,32,512]{4,3,2,1,0:T(8,128)S(1)} %get-tuple-element.25.refs_4_), channel_id=1, source_target_pairs={{0,12},{1,13},{2,14},{3,15},{4,8},{5,9},{6,10},{7,11},{8,4},{9,5},... | collective-permute-start | bytes 4718600 | tf_op jit(solution)/shard_map/ppermute | solution.py:33
  143.4 14.5 %collective-permute-done.21.refs_2_ = f32[4,2,3,32,512]{4,3,2,1,0:T(8,128)S(1)} collective-permute-done((f32[4,2,3,32,512]{4,3,2,1,0:T(8,128)S(1)}, f32[4,2,3,32,512]{4,3,2,1,0:T(8,128)S(1)}, u32[]{:S(2)}, u32[]{:S(2)}) %collective-permute-start.21) | collective-permute-done | bytes 1572896 | tf_op jit(solution)/shard_map/ppermute | solution.py:33
  158.0 1.9 collective-permute-done.24.refs_6_
  159.9 14.9 %collective-permute-done.22.refs_3_ = f32[4,2,3,32,512]{4,3,2,1,0:T(8,128)S(1)} collective-permute-done((f32[4,2,3,32,512]{4,3,2,1,0:T(8,128)S(1)}, f32[4,2,3,32,512]{4,3,2,1,0:T(8,128)S(1)}, u32[]{:S(2)}, u32[]{:S(2)}) %collective-permute-start.22) | collective-permute-done | bytes 1572896 | tf_op jit(solution)/shard_map/ppermute | solution.py:33
  174.8 1.9 collective-permute-done.25.refs_7_
  178.0 1.7 copy-done.6
  179.6 28.7 %update.1 = (f32[4,512,1024]{2,1,0:T(8,128)}, f32[3,512,1024]{2,1,0:T(8,128)}) custom-call(s32[34]{0:T(128)} %pad_add_fusion.tab_ref, f32[3,512,512]{2,1,0:T(8,128)} %copy-done, f32[3,512,512]{2,1,0:T(8,128)} %copy-done.6, f32[4,2,3,32,512]{4,3,2,1,0:T(8,128)} %copy-done.1, f32[4,2,3,32,512]{4,3,2,1,0:T(8,128)} %copy-done.7, ...), custom_call_target="tpu_custom_call" | custom-call | flops 21474836480 | bytes 44040192 | tf_op jit(solution)/shard_map/update/pallas_call | solution.py:382
  (75 shorter events, 18.9 us)
Async XLA Ops:
  1.5 1.3 collective-permute-start
  5.0 10.3 %collective-permute-start.10 = (f32[512,512]{1,0:T(8,128)S(1)}, f32[512,512]{1,0:T(8,128)S(1)}, u32[]{:S(2)}, u32[]{:S(2)}) collective-permute-start(f32[512,512]{1,0:T(8,128)S(1)} %dynamic-slice_bitcast_fusion), channel_id=1, source_target_pairs={{0,16},{1,17},{2,18},{3,19},{4,20},{5,21},{6,22},{7,23},{8,24},{9,... | collective-permute-start | bytes 3145736 | tf_op jit(solution)/shard_map/ppermute | solution.py:33
  5.2 6.0 %collective-permute-start.1 = (f32[2,32,512]{2,1,0:T(8,128)S(1)}, f32[2,32,512]{2,1,0:T(8,128)S(1)}, u32[]{:S(2)}, u32[]{:S(2)}) collective-permute-start(f32[2,32,512]{2,1,0:T(8,128)S(1)} %bitcast_select_fusion.2), channel_id=1, source_target_pairs={{0,32},{1,33},{2,34},{3,35},{4,36},{5,37},{6,38},{7,39},{8,40},{9,... | collective-permute-start | bytes 393224 | tf_op jit(solution)/shard_map/ppermute | solution.py:33
  11.3 9.2 %collective-permute-start.2 = (f32[3,32,512]{2,1,0:T(8,128)S(1)}, f32[3,32,512]{2,1,0:T(8,128)S(1)}, u32[]{:S(2)}, u32[]{:S(2)}) collective-permute-start(f32[3,32,512]{2,1,0:T(8,128)S(1)} %maximum_select_fusion), channel_id=1, source_target_pairs={{0,96},{1,97},{2,98},{3,99},{4,100},{5,101},{6,102},{7,103},{8,104... | collective-permute-start | bytes 589832 | tf_op jit(solution)/shard_map/ppermute | solution.py:33
  17.7 41.9 %collective-permute-start.11 = (f32[512,512]{1,0:T(8,128)}, f32[512,512]{1,0:T(8,128)S(1)}, u32[]{:S(2)}, u32[]{:S(2)}) collective-permute-start(f32[512,512]{1,0:T(8,128)} %bitcast_select_fusion.1), channel_id=1, source_target_pairs={{0,32},{1,33},{2,34},{3,35},{4,36},{5,37},{6,38},{7,39},{8,40},{9,... | collective-permute-start | bytes 3145736 | tf_op jit(solution)/shard_map/ppermute | solution.py:33
  20.6 7.3 %collective-permute-start.5 = (f32[1,3,32,512]{3,2,1,0:T(8,128)S(1)}, f32[1,3,32,512]{3,2,1,0:T(8,128)S(1)}, u32[]{:S(2)}, u32[]{:S(2)}) collective-permute-start(f32[1,3,32,512]{3,2,1,0:T(8,128)S(1)} %select_bitcast_fusion.refs_0_), channel_id=1, source_target_pairs={{0,8},{1,9},{2,10},{3,11},{4,12},{5,13},{6,14},{7,15},{8,0},{9,1},... | collective-permute-start | bytes 589832 | tf_op jit(solution)/shard_map/ppermute | solution.py:33
  23.7 6.3 %collective-permute-start.4 = (f32[1,3,32,512]{3,2,1,0:T(8,128)S(1)}, f32[1,3,32,512]{3,2,1,0:T(8,128)S(1)}, u32[]{:S(2)}, u32[]{:S(2)}) collective-permute-start(f32[1,3,32,512]{3,2,1,0:T(8,128)S(1)} %select_bitcast_fusion.refs_0_), channel_id=1, source_target_pairs={{0,12},{1,13},{2,14},{3,15},{4,0},{5,1},{6,2},{7,3},{8,4},{9,5},{1... | collective-permute-start | bytes 589832 | tf_op jit(solution)/shard_map/ppermute | solution.py:33
  24.8 6.9 %collective-permute-start.3 = (f32[1,3,32,512]{3,2,1,0:T(8,128)S(1)}, f32[1,3,32,512]{3,2,1,0:T(8,128)S(1)}, u32[]{:S(2)}, u32[]{:S(2)}) collective-permute-start(f32[1,3,32,512]{3,2,1,0:T(8,128)S(1)} %select_bitcast_fusion.refs_0_), channel_id=1, source_target_pairs={{0,4},{1,5},{2,6},{3,7},{4,8},{5,9},{6,10},{7,11},{8,12},{9,13},{1... | collective-permute-start | bytes 589832 | tf_op jit(solution)/shard_map/ppermute | solution.py:33
  32.7 13.8 %collective-permute-start.8 = (f32[4,3,32,512]{3,2,1,0:T(8,128)S(1)}, f32[4,3,32,512]{3,2,1,0:T(8,128)}, u32[]{:S(2)}, u32[]{:S(2)}) collective-permute-start(f32[4,3,32,512]{3,2,1,0:T(8,128)S(1)} %shard_map.77.refs_0_), channel_id=1, source_target_pairs={{0,2},{1,3},{2,0},{3,1},{4,6},{5,7},{6,4},{7,5},{8,10},{9,11},{10,... | collective-permute-start | bytes 2359304 | tf_op jit(solution)/shard_map/ppermute | solution.py:33
  36.0 19.2 %collective-permute-start.7 = (f32[4,3,32,512]{3,2,1,0:T(8,128)S(1)}, f32[4,3,32,512]{3,2,1,0:T(8,128)}, u32[]{:S(2)}, u32[]{:S(2)}) collective-permute-start(f32[4,3,32,512]{3,2,1,0:T(8,128)S(1)} %shard_map.77.refs_0_), channel_id=1, source_target_pairs={{0,3},{1,0},{2,1},{3,2},{4,7},{5,4},{6,5},{7,6},{8,11},{9,8},{10,9... | collective-permute-start | bytes 2359304 | tf_op jit(solution)/shard_map/ppermute | solution.py:33
  37.0 18.2 %collective-permute-start.6 = (f32[4,3,32,512]{3,2,1,0:T(8,128)S(1)}, f32[4,3,32,512]{3,2,1,0:T(8,128)}, u32[]{:S(2)}, u32[]{:S(2)}) collective-permute-start(f32[4,3,32,512]{3,2,1,0:T(8,128)S(1)} %shard_map.77.refs_0_), channel_id=1, source_target_pairs={{0,1},{1,2},{2,3},{3,0},{4,5},{5,6},{6,7},{7,4},{8,9},{9,10},{10,1... | collective-permute-start | bytes 2359304 | tf_op jit(solution)/shard_map/ppermute | solution.py:33
  59.5 55.0 %collective-permute-start.9 = (f32[3,512,512]{2,1,0:T(8,128)}, f32[3,512,512]{2,1,0:T(8,128)}, u32[]{:S(2)}, u32[]{:S(2)}) collective-permute-start(f32[3,512,512]{2,1,0:T(8,128)} %pack.1.own), channel_id=1, source_target_pairs={{0,16},{1,17},{2,18},{3,19},{4,20},{5,21},{6,22},{7,23},{8,24},{9,... | collective-permute-start | bytes 9437192 | tf_op jit(solution)/shard_map/ppermute | solution.py:33
  62.1 25.4 %collective-permute-start.12 = (f32[512,512]{1,0:T(8,128)}, f32[512,512]{1,0:T(8,128)}, u32[]{:S(2)}, u32[]{:S(2)}) collective-permute-start(f32[512,512]{1,0:T(8,128)} %fusion), channel_id=1, source_target_pairs={{0,32},{1,33},{2,34},{3,35},{4,36},{5,37},{6,38},{7,39},{8,40},{9,... | collective-permute-start | bytes 3145736 | tf_op jit(solution)/shard_map/ppermute | solution.py:33
  88.9 25.5 %copy-start.3 = (f32[3,512]{1,0:T(4,128)S(1)}, f32[3,512]{1,0:T(4,128)}, u32[]{:S(2)}) copy-start(f32[3,512]{1,0:T(4,128)} %piv.1) | copy-start | bytes 18436
  88.9 16.1 %collective-permute-start.13 = (f32[512,512]{1,0:T(8,128)S(1)}, f32[512,512]{1,0:T(8,128)S(1)}, u32[]{:S(2)}, u32[]{:S(2)}) collective-permute-start(f32[512,512]{1,0:T(8,128)S(1)} %broadcast_select_fusion), channel_id=1, source_target_pairs={{0,32},{1,33},{2,34},{3,35},{4,36},{5,37},{6,38},{7,39},{8,40},{9,... | collective-permute-start | bytes 3145736 | tf_op jit(solution)/shard_map/ppermute | solution.py:33
  90.2 7.9 %collective-permute-start.17 = (f32[1,2,3,32,512]{4,3,2,1,0:T(8,128)S(1)}, f32[1,2,3,32,512]{4,3,2,1,0:T(8,128)S(1)}, u32[]{:S(2)}, u32[]{:S(2)}) collective-permute-start(f32[1,2,3,32,512]{4,3,2,1,0:T(8,128)S(1)} %get-tuple-element.28.refs_2_), channel_id=1, source_target_pairs={{0,1},{1,0},{2,3},{3,2},{4,5},{5,4},{6,7},{7,6},{8,9},{9,8},{10,11... | collective-permute-start | bytes 1179656 | tf_op jit(solution)/shard_map/ppermute | solution.py:33
  91.6 7.8 %collective-permute-start.16 = (f32[1,2,3,32,512]{4,3,2,1,0:T(8,128)S(1)}, f32[1,2,3,32,512]{4,3,2,1,0:T(8,128)S(1)}, u32[]{:S(2)}, u32[]{:S(2)}) collective-permute-start(f32[1,2,3,32,512]{4,3,2,1,0:T(8,128)S(1)} %get-tuple-element.29.refs_0_), channel_id=1, source_target_pairs={{0,4},{1,5},{2,6},{3,7},{4,0},{5,1},{6,2},{7,3},{8,12},{9,13},{10,... | collective-permute-start | bytes 1179656 | tf_op jit(solution)/shard_map/ppermute | solution.py:33
  100.2 13.3 %collective-permute-start.18 = (f32[2,2,3,32,512]{4,3,2,1,0:T(8,128)S(1)}, f32[2,2,3,32,512]{4,3,2,1,0:T(8,128)S(1)}, u32[]{:S(2)}, u32[]{:S(2)}) collective-permute-start(f32[2,2,3,32,512]{4,3,2,1,0:T(8,128)S(1)} %get-tuple-element.22.refs_0_), channel_id=1, source_target_pairs={{0,12},{1,13},{2,14},{3,15},{4,8},{5,9},{6,10},{7,11},{8,4},{9,5},... | collective-permute-start | bytes 2359304 | tf_op jit(solution)/shard_map/ppermute | solution.py:33
  100.3 13.3 %collective-permute-start.19 = (f32[2,2,3,32,512]{4,3,2,1,0:T(8,128)S(1)}, f32[2,2,3,32,512]{4,3,2,1,0:T(8,128)S(1)}, u32[]{:S(2)}, u32[]{:S(2)}) collective-permute-start(f32[2,2,3,32,512]{4,3,2,1,0:T(8,128)S(1)} %get-tuple-element.23.refs_2_), channel_id=1, source_target_pairs={{0,3},{1,2},{2,1},{3,0},{4,7},{5,6},{6,5},{7,4},{8,11},{9,10},{10,... | collective-permute-start | bytes 2359304 | tf_op jit(solution)/shard_map/ppermute | solution.py:33
  105.0 18.9 %collective-permute-start.14 = (f32[512,512]{1,0:T(8,128)S(1)}, f32[512,512]{1,0:T(8,128)S(1)}, u32[]{:S(2)}, u32[]{:S(2)}) collective-permute-start(f32[512,512]{1,0:T(8,128)S(1)} %collective-permute-done.13.r3), channel_id=1, source_target_pairs={{0,32},{1,33},{2,34},{3,35},{4,36},{5,37},{6,38},{7,39},{8,40},{9,... | collective-permute-start | bytes 3145736 | tf_op jit(solution)/shard_map/ppermute | solution.py:33
  113.8 22.6 %copy-start.1 = (f32[4,2,3,32,512]{4,3,2,1,0:T(8,128)}, f32[4,2,3,32,512]{4,3,2,1,0:T(8,128)S(1)}, u32[]{:S(2)}) copy-start(f32[4,2,3,32,512]{4,3,2,1,0:T(8,128)S(1)} %get-tuple-element.24.refs_0_) | copy-start | bytes 4718596
  113.8 24.5 %copy-start.2 = (f32[4,2,3,32,512]{4,3,2,1,0:T(8,128)}, f32[4,2,3,32,512]{4,3,2,1,0:T(8,128)S(1)}, u32[]{:S(2)}) copy-start(f32[4,2,3,32,512]{4,3,2,1,0:T(8,128)S(1)} %get-tuple-element.25.refs_4_) | copy-start | bytes 4718596
  113.8 27.2 %collective-permute-start.20 = (f32[4,2,3,32,512]{4,3,2,1,0:T(8,128)S(1)}, f32[4,2,3,32,512]{4,3,2,1,0:T(8,128)S(1)}, u32[]{:S(2)}, u32[]{:S(2)}) collective-permute-start(f32[4,2,3,32,512]{4,3,2,1,0:T(8,128)S(1)} %get-tuple-element.24.refs_0_), channel_id=1, source_target_pairs={{0,1},{1,0},{2,3},{3,2},{4,5},{5,4},{6,7},{7,6},{8,9},{9,8},{10,11... | collective-permute-start | bytes 4718600 | tf_op jit(solution)/shard_map/ppermute | solution.py:33
  114.5 27.1 %collective-permute-start.23 = (f32[4,2,3,32,512]{4,3,2,1,0:T(8,128)S(1)}, f32[4,2,3,32,512]{4,3,2,1,0:T(8,128)}, u32[]{:S(2)}, u32[]{:S(2)}) collective-permute-start(f32[4,2,3,32,512]{4,3,2,1,0:T(8,128)S(1)} %get-tuple-element.25.refs_4_), channel_id=1, source_target_pairs={{0,4},{1,5},{2,6},{3,7},{4,0},{5,1},{6,2},{7,3},{8,12},{9,13},{10,... | collective-permute-start | bytes 4718600 | tf_op jit(solution)/shard_map/ppermute | solution.py:33
  134.7 43.3 %copy-start = (f32[3,512,512]{2,1,0:T(8,128)}, f32[3,512,512]{2,1,0:T(8,128)S(1)}, u32[]{:S(2)}) copy-start(f32[3,512,512]{2,1,0:T(8,128)S(1)} %solve.1.xa_hbm) | copy-start | bytes 9437188
  134.7 43.2 %collective-permute-start.15 = (f32[3,512,512]{2,1,0:T(8,128)S(1)}, f32[3,512,512]{2,1,0:T(8,128)S(1)}, u32[]{:S(2)}, u32[]{:S(2)}) collective-permute-start(f32[3,512,512]{2,1,0:T(8,128)S(1)} %solve.1.xa_hbm), channel_id=1, source_target_pairs={{0,16},{1,17},{2,18},{3,19},{4,20},{5,21},{6,22},{7,23},{8,24},{9,... | collective-permute-start | bytes 9437192 | tf_op jit(solution)/shard_map/ppermute | solution.py:33
  136.4 21.6 %collective-permute-start.21 = (f32[4,2,3,32,512]{4,3,2,1,0:T(8,128)S(1)}, f32[4,2,3,32,512]{4,3,2,1,0:T(8,128)S(1)}, u32[]{:S(2)}, u32[]{:S(2)}) collective-permute-start(f32[4,2,3,32,512]{4,3,2,1,0:T(8,128)S(1)} %get-tuple-element.24.refs_0_), channel_id=1, source_target_pairs={{0,3},{1,2},{2,1},{3,0},{4,7},{5,6},{6,5},{7,4},{8,11},{9,10},{10,... | collective-permute-start | bytes 4718600 | tf_op jit(solution)/shard_map/ppermute | solution.py:33
  138.3 21.6 %collective-permute-start.24 = (f32[4,2,3,32,512]{4,3,2,1,0:T(8,128)S(1)}, f32[4,2,3,32,512]{4,3,2,1,0:T(8,128)S(1)}, u32[]{:S(2)}, u32[]{:S(2)}) collective-permute-start(f32[4,2,3,32,512]{4,3,2,1,0:T(8,128)S(1)} %get-tuple-element.25.refs_4_), channel_id=1, source_target_pairs={{0,12},{1,13},{2,14},{3,15},{4,8},{5,9},{6,10},{7,11},{8,4},{9,5},... | collective-permute-start | bytes 4718600 | tf_op jit(solution)/shard_map/ppermute | solution.py:33
  141.0 33.9 %copy-start.7 = (f32[4,2,3,32,512]{4,3,2,1,0:T(8,128)}, f32[4,2,3,32,512]{4,3,2,1,0:T(8,128)S(1)}, u32[]{:S(2)}) copy-start(f32[4,2,3,32,512]{4,3,2,1,0:T(8,128)S(1)} %collective-permute-done.20.refs_1_) | copy-start | bytes 4718596
  141.0 33.9 %collective-permute-start.22 = (f32[4,2,3,32,512]{4,3,2,1,0:T(8,128)S(1)}, f32[4,2,3,32,512]{4,3,2,1,0:T(8,128)S(1)}, u32[]{:S(2)}, u32[]{:S(2)}) collective-permute-start(f32[4,2,3,32,512]{4,3,2,1,0:T(8,128)S(1)} %collective-permute-done.20.refs_1_), channel_id=1, source_target_pairs={{0,3},{1,2},{2,1},{3,0},{4,7},{5,6},{6,5},{7,4},{8,11},{9,10},{10,... | collective-permute-start | bytes 4718600 | tf_op jit(solution)/shard_map/ppermute | solution.py:33
  141.6 35.2 %collective-permute-start.25 = (f32[4,2,3,32,512]{4,3,2,1,0:T(8,128)}, f32[4,2,3,32,512]{4,3,2,1,0:T(8,128)S(1)}, u32[]{:S(2)}, u32[]{:S(2)}) collective-permute-start(f32[4,2,3,32,512]{4,3,2,1,0:T(8,128)} %collective-permute-done.23.refs_5_), channel_id=1, source_target_pairs={{0,12},{1,13},{2,14},{3,15},{4,8},{5,9},{6,10},{7,11},{8,4},{9,5},... | collective-permute-start | bytes 4718600 | tf_op jit(solution)/shard_map/ppermute | solution.py:33
  158.0 20.0 %copy-start.8 = (f32[4,2,3,32,512]{4,3,2,1,0:T(8,128)}, f32[4,2,3,32,512]{4,3,2,1,0:T(8,128)S(1)}, u32[]{:S(2)}) copy-start(f32[4,2,3,32,512]{4,3,2,1,0:T(8,128)S(1)} %collective-permute-done.21.refs_2_) | copy-start | bytes 4718596
  (8 other events, 78.4 us)
